TPU v7x, 32 devices: a whole 2x2x4 slice. The times are simulated.
32 devices in a mesh: az: 2 (over x), rad: 4 (over y, core), ax: 4 (over z).
Axes of the slice: x: 2, y: 2, z: 4, core: 2. Of those that a mesh axis runs over, the one named last changes fastest.
Arguments:
- velocity: float32 [3, 32, 1536, 512], P(None, 'ax', 'az', 'rad'), may hold values from -40 to 40, as said below
- cutoff: int32 [512], replicated, may hold values from 2 to 511, as said below
- shells: int32 [3], replicated, may hold values from 128 to 256, as said below
Outputs:
- filtered: float32 [3, 32, 1536, 512], P(None, 'ax', 'az', 'rad')
- viscosity: float32 [32, 1536, 512], P('ax', 'az', 'rad')
- coefficient: float32 [512], P('rad')
Inputs may be any that keep to these rules, and one draw needn't show every extreme that they name: `velocity`: components in the order axial, radial, azimuthal. cutoff of shell k is the highest azimuthal mode kept there; 511 is reached. `shells`: one count per velocity component; one of the three equals 256.
All inputs are finite; a program needn't handle non-finite values.
Results may differ from a plain program's by a relative error of at most 0.0003.
Values sent between devices are 32-bit elements; how exact they have to be, the bound alone decides.
A program may use at most 384 MiB of HBM per device.

v0:
```python
import math

import jax
import jax.numpy as jnp
from jax import lax
from jax.sharding import PartitionSpec as P

MODES = 512


index_pairs = ((0, 0), (1, 1), (2, 2), (0, 1), (0, 2), (1, 2))


def extended(block, sides, width, periodic):
    for axis, dim in sides:
        count = lax.axis_size(axis)
        forward = [(i, i + 1) for i in range(count - 1)]
        if periodic:
            forward.append((count - 1, 0))
        backward = [(target, source) for source, target in forward]
        low = lax.ppermute(
            lax.slice_in_dim(block, block.shape[dim] - width, None, axis=dim), axis, forward
        )
        high = lax.ppermute(lax.slice_in_dim(block, 0, width, axis=dim), axis, backward)
        block = jnp.concatenate([low, block, high], axis=dim)
    return block


def spacing_of(shell_pos, azimuths):
    return jnp.maximum(shell_pos * (2.0 * math.pi / azimuths), 1.0)


def strain(source, lower, upper, shell_pos, spacing):
    center = source[:, 1:-1, 1:-1, :]
    along_z = (source[:, 2:, 1:-1, :] - source[:, :-2, 1:-1, :]) * 0.5
    along_t = (source[:, 1:-1, 2:, :] - source[:, 1:-1, :-2, :]) * (0.5 / spacing)
    above = jnp.concatenate([center[:, :, :, 1:], upper], axis=3)
    below = jnp.concatenate([lower, center[:, :, :, :-1]], axis=3)
    along_r = (above - below) * 0.5
    tensor = jnp.stack(
        [
            along_z[0],
            along_r[1],
            along_t[2] + center[1] / shell_pos,
            0.5 * (along_r[0] + along_z[1]),
            0.5 * (along_t[0] + along_z[2]),
            0.5 * (along_r[2] - center[2] / shell_pos + along_t[1]),
        ]
    )
    magnitude = jnp.sqrt(
        2.0 * jnp.sum(tensor[:3] ** 2, axis=0) + 4.0 * jnp.sum(tensor[3:] ** 2, axis=0)
    )
    return (tensor, magnitude)


def smooth(source):
    partial_value = 0.25 * source[:, :-2] + 0.5 * source[:, 1:-1] + 0.25 * source[:, 2:]
    return (
        0.25 * partial_value[:, :, :-2]
        + 0.5 * partial_value[:, :, 1:-1]
        + 0.25 * partial_value[:, :, 2:]
    )


def outer_terms(source):
    return jnp.stack([source[first] * source[second] for first, second in index_pairs])


def contract(left_side, right_side):
    return jnp.sum(left_side[:3] * right_side[:3], axis=0) + 2.0 * jnp.sum(
        left_side[3:] * right_side[3:], axis=0
    )


def identity_sums(hat_products, hat_model, hat_velocity, hat_tensor, hat_magnitude, spacing):
    leonard = hat_products - outer_terms(hat_velocity)
    trace_third = (leonard[0] + leonard[1] + leonard[2]) / 3.0
    leonard = jnp.concatenate([leonard[:3] - trace_third, leonard[3:]])
    scale_sq = jnp.power(spacing, 2.0 / 3.0)
    model_tensor = 2.0 * scale_sq * (hat_model - 4.0 * hat_magnitude * hat_tensor)
    numerator = jnp.sum(contract(leonard, model_tensor), axis=(0, 1))
    denominator = jnp.sum(contract(model_tensor, model_tensor), axis=(0, 1))
    return (numerator, denominator)


def pad_around(source, rim_depth):
    return extended(source, (("az", 2), ("ax", 1)), rim_depth, True)


def edge_shells(source):
    edges = jnp.concatenate([source[:, :, :, :1], source[:, :, :, -1:]], axis=3)
    rimmed = extended(edges, (("rad", 3),), 1, False)
    return (rimmed[:, :, :, :1], rimmed[:, :, :, 3:])


def pad_all(source):
    lower, upper = edge_shells(source)
    return (pad_around(source, 1), lower, upper)


def mode_table(column_ids, azimuths):
    angles = column_ids[:, None] * jnp.arange(MODES, dtype=jnp.int32)[None, :] % azimuths
    phases = angles.astype(jnp.float32) * (2.0 * math.pi / azimuths)
    return jnp.concatenate([jnp.cos(phases), jnp.sin(phases)], axis=1)


def mode_scaling(first_shell, radial, shells, cutoff, azimuths):
    shell_ids = first_shell + jnp.arange(radial, dtype=jnp.int32)
    cutoffs = lax.dynamic_slice_in_dim(cutoff, first_shell, radial)
    live_rows = shell_ids[None, :] < shells[:, None]
    mode_index = jnp.concatenate(
        [jnp.arange(MODES, dtype=jnp.int32), jnp.arange(MODES, dtype=jnp.int32)]
    )
    weight = jnp.where(mode_index == 0, 1.0, 2.0).astype(jnp.float32) / azimuths
    kept_modes = jnp.where(mode_index[:, None] <= cutoffs[None, :], weight[:, None], 0.0)
    scaling = jnp.where(live_rows[:, None, :], kept_modes[None], 0.0)
    return (scaling, live_rows)


def polar_filter(block_rows, first_shell, shells, cutoff):
    azimuths = block_rows.shape[2]
    radial = block_rows.shape[3]
    scaling, live_rows = mode_scaling(first_shell, radial, shells, cutoff, azimuths)
    fourier = mode_table(jnp.arange(azimuths, dtype=jnp.int32), azimuths)
    spectrum = jnp.einsum("cztr,tm->czmr", block_rows, fourier, precision=lax.Precision.HIGHEST)
    rebuilt = jnp.einsum(
        "czmr,tm->cztr", spectrum * scaling[:, None], fourier, precision=lax.Precision.HIGHEST
    )
    return jnp.where(live_rows[:, None, None, :], rebuilt, block_rows)


def azimuth_filter(block_rows, first_shell, shells, cutoff, inner_side):
    azimuth_rows = lax.all_to_all(block_rows, "az", split_axis=1, concat_axis=2, tiled=True)
    processed = lax.cond(
        inner_side,
        lambda values: polar_filter(values, first_shell, shells, cutoff),
        lambda values: values,
        azimuth_rows,
    )
    return lax.all_to_all(processed, "az", split_axis=2, concat_axis=1, tiled=True)


def polar_step(velocity, cutoff, shells, first_shell):
    chain_size = lax.axis_size("rad")
    inner_side = lax.axis_index("rad") < chain_size // 2
    return azimuth_filter(velocity, first_shell, shells, cutoff, inner_side)


def finish(numerator, denominator, magnitude, spacing_int, surface_cells):
    totals = lax.psum((numerator, denominator), ("az", "ax"))
    coefficient = totals[0] / surface_cells / (totals[1] / surface_cells + 1e-06)
    viscosity = coefficient * jnp.power(spacing_int, 2.0 / 3.0) * magnitude
    return (coefficient, viscosity)


def local(velocity, cutoff, shells):
    planes = velocity.shape[1]
    columns = velocity.shape[2]
    radial = velocity.shape[3]
    azimuths = columns * lax.axis_size("az")
    surface_cells = planes * lax.axis_size("ax") * azimuths
    first_shell = lax.axis_index("rad") * radial
    shell_int = first_shell.astype(jnp.float32) + jnp.arange(radial, dtype=jnp.float32) + 0.5
    spacing_int = spacing_of(shell_int, azimuths)
    bordered, lower, upper = pad_all(velocity)
    tensor, magnitude = strain(bordered, lower, upper, shell_int, spacing_int)
    stacked = jnp.concatenate([velocity, outer_terms(velocity), magnitude * tensor])
    filtered_terms = smooth(pad_around(stacked, 1))
    hat_velocity = filtered_terms[:3]
    hat_bordered, hat_lower, hat_upper = pad_all(hat_velocity)
    hat_tensor, hat_magnitude = strain(hat_bordered, hat_lower, hat_upper, shell_int, spacing_int)
    numerator, denominator = identity_sums(
        filtered_terms[3:9],
        filtered_terms[9:],
        hat_velocity,
        hat_tensor,
        hat_magnitude,
        spacing_int,
    )
    coefficient, viscosity = finish(numerator, denominator, magnitude, spacing_int, surface_cells)
    filtered = polar_step(velocity, cutoff, shells, first_shell)
    return (filtered, viscosity, coefficient)


def solution(mesh):
    in_specs = (P(None, "ax", "az", "rad"), P(), P())
    out_specs = (P(None, "ax", "az", "rad"), P("ax", "az", "rad"), P("rad"))
    return jax.shard_map(local, mesh=mesh, in_specs=in_specs, out_specs=out_specs, check_vma=False)
```

profile of v0, /device:TPU:0, one launch (start us, length us, event | category | flops | bytes accessed | tf_op | source)
XLA Modules:
  0.0 1004.4 jit_solution(9031836514831135580)
XLA Ops:
  0.6 15.9 %constant_dynamic-update-slice_fusion.6 = (f32[15,8,768,128]{3,1,2,0:T(8,128)}, f32[3,8,768,128]{3,1,2,0:T(8,128)}) fusion(f32[3,8,768,128]{3,2,1,0:T(8,128)} %param.5), kind=kLoop, calls=%fused_computation.135 | loop fusion | bytes 28311552
  20.3 11.8 %fusion.57 = (f32[3,8,768,1]{3,2,1,0:T(8,128)}, f32[3,8,768,1]{3,2,1,0:T(8,128)}) fusion(f32[3,8,768,128]{3,2,1,0:T(8,128)} %param.5), kind=kLoop, calls=%fused_computation.156 | loop fusion | bytes 294912 | tf_op jit(solution)/shard_map/slice | solution.py:91
  50.8 13.2 %fusion.58 = (f32[3,8,768,127]{3,1,2,0:T(8,128)}, f32[3,8,768,127]{3,1,2,0:T(8,128)}) fusion(f32[3,8,768,128]{3,1,2,0:T(8,128)} %get-tuple-element.85), kind=kLoop, calls=%fused_computation.157 | loop fusion | bytes 37453824 | tf_op jit(solution)/shard_map/slice | solution.py:38
  100.2 17.8 %fusion.28 = f32[3,8,768,128]{3,1,2,0:T(8,128)} fusion(f32[3,8,768,1]{3,1,2,0:T(8,128)} %copy.95, f32[3,8,768,127]{3,1,2,0:T(8,128)} %get-tuple-element.91, f32[3,8,768,127]{3,1,2,0:T(8,128)} %get-tuple-element.90, f32[3,8,768,1]{3,1,2,0:T(8,128)} %copy.98), kind=kLoop, calls=%fused_computation.71 | loop fusion | flops 9437184 | bytes 28311552 | tf_op jit(solution)/shard_map/mul | solution.py:39
  134.9 21.0 %fusion.34 = f32[3,8,768,128]{3,1,2,0:T(8,128)} fusion(f32[3,8,768,128]{3,2,1,0:T(8,128)} %get-tuple-element.74, f32[3,8,768,128]{3,2,1,0:T(8,128)} %get-tuple-element.73), kind=kLoop, calls=%fused_computation.83 | loop fusion | flops 4718592 | bytes 28311552 | tf_op jit(solution)/shard_map/mul | solution.py:35
  218.1 15.3 %multiply_dynamic-update-slice_fusion = f32[15,8,768,128]{3,1,2,0:T(8,128)} fusion(f32[15,8,768,128]{3,1,2,0:T(8,128)} %get-tuple-element.81, f32[6,8,768,128]{3,1,2,0:T(8,128)} %get-tuple-element.45, f32[8,768,128]{2,0,1:T(8,128)} %copy.103), kind=kLoop, calls=%fused_computation.42 | loop fusion | flops 4718592 | bytes 40894464 | tf_op jit(solution)/shard_map/concatenate | solution.py:167
  240.1 30.9 %pad_maximum_fusion.6 = f32[15,8,770,128]{3,1,2,0:T(8,128)} fusion(f32[15,8,1,128]{3,1,2,0:T(8,128)S(1)} %collective-permute-done.7, f32[15,8,768,128]{3,1,2,0:T(8,128)} %multiply_dynamic-update-slice_fusion, f32[15,8,1,128]{3,1,2,0:T(8,128)S(1)} %collective-permute-done.6), kind=kLoop, calls=%fused_computation.33 | loop fusion | flops 23654400 | bytes 94617600 | tf_op jit(solution)/shard_map/concatenate | solution.py:25
  270.9 31.9 %fusion.49 = (f32[15,1,770,128]{3,1,2,0:T(1,128)}, f32[15,1,770,128]{3,1,2,0:T(1,128)S(1)}) fusion(f32[15,8,770,128]{3,1,2,0:T(8,128)} %pad_maximum_fusion.6), kind=kLoop, calls=%fused_computation.148 | loop fusion | bytes 23654400 | tf_op jit(solution)/shard_map/slice | solution.py:22
  328.2 101.8 %all-to-all-done = f32[3,8,768,128]{3,2,0,1:T(8,128)} async-done(((f32[3,8,768,128]{3,2,0,1:T(8,128)}), f32[3,8,768,128]{3,2,0,1:T(8,128)}, u32[]{:S(2)}, u32[]{:S(2)}) %all-to-all-start) | async-done | bytes 9437216 | tf_op jit(solution)/shard_map/all_to_all | solution.py:133
  438.3 84.4 %conditional.1 = (f32[3,4,1536,128]{3,2,1,0:T(8,128)}) conditional(s32[]{:T(128)} %convert_element_type.11, f32[3,4,1536,128]{3,2,1,0:T(8,128)} %bitcast.7, (s32[]{:T(128)}, s32[3]{0:T(128)S(1)}, f32[3,4,1536,128]{3,2,1,0:T(8,128)}, s32[512]{0:T(512)}) %tuple.56), branch_computations={%region_0.0_spmd, %region_1.0_spmd} | conditional | flops 57996873728 | bytes 63989436 | solution.py:134
  440.0 12.6 %fusion.7 = (f32[1536,512]{0,1:T(8,128)S(1)}, f32[1536,512]{0,1:T(8,128)S(1)}) fusion(), kind=kLoop, calls=%fused_computation.12 | loop fusion | flops 7077888 | bytes 6291456 | tf_op jit(solution)/shard_map/cond/branch_1_fun/sin | solution.py:104
  452.7 34.2 %fusion.1 = f32[1024,3,4,128]{3,0,2,1:T(8,128)S(1)} fusion(f32[3,4,1536,128]{3,2,1,0:T(8,128)} %get-tuple-element.14, f32[1536,512]{0,1:T(8,128)S(1)} %get-tuple-element.53, f32[1536,512]{0,1:T(8,128)S(1)} %get-tuple-element.54), kind=kOutput, calls=%fused_computation.4 | convolution fusion | flops 28992602112 | bytes 22020096 | tf_op jit(solution)/shard_map/cond/branch_1_fun/cztr,tm->czmr/dot_general | solution.py:125
  486.9 35.4 %bitcast_select_fusion = f32[3,4,1536,128]{3,2,1,0:T(8,128)} fusion(f32[3,4,1536,128]{3,2,1,0:T(8,128)} %get-tuple-element.14, pred[3,128]{1,0:T(4,128)(4,1)S(1)} %broadcast_compare_fusion, f32[1024,3,4,128]{3,0,2,1:T(8,128)S(1)} %fusion.1, f32[1536,512]{0,1:T(8,128)S(1)} %get-tuple-element.53, f32[1536,512]{0,1:T(8,128)S(1)} %get-tuple-element.54, ...), kind=kOutput, calls=%fused_computation | convolution fusion | flops 28996534272 | bytes 33030528 | tf_op jit(solution)/shard_map/cond/branch_1_fun/czmr,tm->cztr/dot_general | solution.py:126
  522.7 17.1 %copy.82 = f32[3,4,1536,128]{3,1,0,2:T(4,128)} copy(f32[3,4,1536,128]{3,2,1,0:T(8,128)} %get-tuple-element.96) | data formatting | bytes 18874368 | tf_op jit(solution)/shard_map/cond | solution.py:134
  554.7 13.5 %collective-permute-done.9 = f32[15,1,770,128]{3,2,1,0:T(8,128)} collective-permute-done((f32[15,1,770,128]{3,2,1,0:T(8,128)}, f32[15,1,770,128]{3,2,1,0:T(8,128)}, u32[]{:S(2)}, u32[]{:S(2)}) %collective-permute-start.9) | collective-permute-done | bytes 5913632 | tf_op jit(solution)/shard_map/ppermute | solution.py:24
  575.7 65.1 %fusion.13 = f32[15,8,770,128]{3,1,2,0:T(8,128)} fusion(f32[15,1,770,128]{3,1,2,0:T(1,128)S(1)} %copy.108, f32[15,8,1,128]{3,1,2,0:T(8,128)S(1)} %collective-permute-done.7, f32[15,8,768,128]{3,1,2,0:T(8,128)} %multiply_dynamic-update-slice_fusion, f32[15,8,1,128]{3,1,2,0:T(8,128)S(1)} %collective-permute-done.6, f32[15,1,770,128]{3,1,2,0:T(1,128)S(1)} %copy.106), kind=kLoop, calls=%fused_computation.25 | loop fusion | flops 153753600 | bytes 106444800 | tf_op jit(solution)/shard_map/add | solution.py:57
  640.8 59.7 %fusion.16 = f32[15,8,768,128]{3,1,2,0:T(8,128)} fusion(f32[15,8,770,128]{3,1,2,0:T(8,128)} %fusion.13), kind=kLoop, calls=%fused_computation.35 | loop fusion | flops 58982400 | bytes 188743680 | tf_op jit(solution)/shard_map/add | solution.py:59
  701.2 11.9 %fusion.50 = (f32[3,8,768,1]{3,1,2,0:T(8,128)}, f32[3,8,768,1]{3,1,2,0:T(8,128)}) fusion(f32[15,8,768,128]{3,1,2,0:T(8,128)} %fusion.16), kind=kLoop, calls=%fused_computation.149 | loop fusion | bytes 294912 | tf_op jit(solution)/shard_map/slice | solution.py:91
  713.2 11.8 %fusion.51 = (f32[3,8,768,127]{3,1,2,0:T(8,128)}, f32[3,8,768,127]{3,1,2,0:T(8,128)}) fusion(f32[15,8,768,128]{3,1,2,0:T(8,128)} %fusion.16), kind=kLoop, calls=%fused_computation.150 | loop fusion | bytes 37453824 | tf_op jit(solution)/shard_map/slice | solution.py:38
  786.7 17.8 %fusion.31 = f32[3,8,768,128]{3,1,2,0:T(8,128)} fusion(f32[3,8,768,1]{3,1,2,0:T(8,128)} %copy.114, f32[3,8,768,127]{3,1,2,0:T(8,128)} %get-tuple-element.64, f32[3,8,768,127]{3,1,2,0:T(8,128)} %get-tuple-element.63, f32[3,8,768,1]{3,1,2,0:T(8,128)} %copy.116), kind=kLoop, calls=%fused_computation.77 | loop fusion | flops 9437184 | bytes 28311552 | tf_op jit(solution)/shard_map/mul | solution.py:39
  804.5 14.4 %collective-permute-done.12 = f32[3,1,770,128]{3,2,1,0:T(8,128)S(1)} collective-permute-done((f32[3,1,770,128]{3,2,1,0:T(8,128)S(1)}, f32[3,1,770,128]{3,2,1,0:T(8,128)S(1)}, u32[]{:S(2)}, u32[]{:S(2)}) %collective-permute-start.12) | collective-permute-done | bytes 1182752 | tf_op jit(solution)/shard_map/ppermute | solution.py:24
  890.0 37.4 %fusion.18 = (f32[6,8,768,128]{3,1,2,0:T(8,128)}, f32[6,8,768,128]{3,1,2,0:T(8,128)}) fusion(f32[15,8,768,128]{3,1,2,0:T(8,128)} %fusion.16, f32[6,8,768,128]{3,1,2,0:T(8,128)} %get-tuple-element.37, f32[8,768,128]{2,0,1:T(8,128)S(1)} %copy.119, f32[128]{0:T(128)S(1)} %copy-done.8, f32[6,8,768,128]{3,1,2,0:T(8,128)} %get-tuple-element.59), kind=kLoop, calls=%fused_computation.40 | loop fusion | flops 18874368 | bytes 116392448 | tf_op jit(solution)/shard_map/mul | solution.py:80
  931.6 18.2 %fusion.19 = (f32[8,768,128]{2,0,1:T(8,128)}, f32[8,768,128]{2,0,1:T(8,128)}, f32[8,768,128]{2,0,1:T(8,128)S(1)}, f32[8,768,128]{2,0,1:T(8,128)}) fusion(f32[6,8,768,128]{3,1,2,0:T(8,128)} %get-tuple-element.58, f32[6,8,768,128]{3,1,2,0:T(8,128)} %get-tuple-element.57, f32[8,768,128]{2,0,1:T(8,128)S(1)} %fusion.39), kind=kLoop, calls=%fused_computation.44 | loop fusion | flops 18087936 | bytes 53477376 | tf_op jit(solution)/shard_map/reduce_sum | solution.py:70
  971.0 18.4 %all-reduce = (f32[128]{0:T(128)S(1)}, f32[128]{0:T(128)S(1)}) all-reduce(f32[128]{0:T(128)S(1)} %add_reduce_fusion, f32[128]{0:T(128)S(1)} %add_reduce_fusion.1), channel_id=1, replica_groups=mesh['az'=2,'rad'=4,'ax'=4] {'az','ax'}, use_global_device_ids=true, to_apply=%region_13.14 | all-reduce | flops 256 | bytes 2048 | tf_op jit(solution)/shard_map/psum | solution.py:150
  (182 shorter events, 374.9 us)
Async XLA Ops:
  17.3 52.4 %collective-permute-start = (f32[3,8,1,128]{3,1,2,0:T(8,128)S(1)}, f32[3,8,1,128]{3,1,2,0:T(8,128)S(1)}, u32[]{:S(2)}, u32[]{:S(2)}) collective-permute-start(f32[3,8,1,128]{3,1,2,0:T(8,128)S(1)} %get-tuple-element.92), channel_id=1, source_target_pairs={{0,16},{16,0},{1,17},{17,1},{2,18},{18,2},{3,19},{19,3},{4,20},{20... | collective-permute-start | bytes 36872 | tf_op jit(solution)/shard_map/ppermute | solution.py:21
  20.2 49.4 %collective-permute-start.1 = (f32[3,8,1,128]{3,1,2,0:T(8,128)S(1)}, f32[3,8,1,128]{3,1,2,0:T(8,128)S(1)}, u32[]{:S(2)}, u32[]{:S(2)}) collective-permute-start(f32[3,8,1,128]{3,1,2,0:T(8,128)S(1)} %get-tuple-element.93), channel_id=1, source_target_pairs={{16,0},{0,16},{17,1},{1,17},{18,2},{2,18},{19,3},{3,19},{20,4},{4,... | collective-permute-start | bytes 36872 | tf_op jit(solution)/shard_map/ppermute | solution.py:24
  38.4 48.7 %collective-permute-start.4 = (f32[3,8,768,1]{2,1,3,0:T(8,128)S(1)}, f32[3,8,768,1]{2,1,3,0:T(8,128)}, u32[]{:S(2)}, u32[]{:S(2)}) collective-permute-start(f32[3,8,768,1]{2,1,3,0:T(8,128)S(1)} %copy.138), channel_id=1, source_target_pairs={{4,0},{8,4},{12,8},{5,1},{9,5},{13,9},{6,2},{10,6},{14,10},{7,3},{... | collective-permute-start | bytes 221192 | tf_op jit(solution)/shard_map/ppermute | solution.py:24
  46.9 46.7 %collective-permute-start.5 = (f32[3,8,768,1]{2,1,3,0:T(8,128)}, f32[3,8,768,1]{2,1,3,0:T(8,128)}, u32[]{:S(2)}, u32[]{:S(2)}) collective-permute-start(f32[3,8,768,1]{2,1,3,0:T(8,128)} %copy.139), channel_id=1, source_target_pairs={{0,4},{4,8},{8,12},{1,5},{5,9},{9,13},{2,6},{6,10},{10,14},{3,7},{... | collective-permute-start | bytes 221192 | tf_op jit(solution)/shard_map/ppermute | solution.py:21
  69.9 48.1 %collective-permute-start.2 = (f32[3,1,770,128]{3,2,1,0:T(8,128)S(1)}, f32[3,1,770,128]{3,2,1,0:T(8,128)}, u32[]{:S(2)}, u32[]{:S(2)}) collective-permute-start(f32[3,1,770,128]{3,2,1,0:T(8,128)S(1)} %get-tuple-element.75), channel_id=1, source_target_pairs={{1,0},{2,1},{3,2},{0,3},{5,4},{6,5},{7,6},{4,7},{9,8},{10,9},{11,1... | collective-permute-start | bytes 3548168 | tf_op jit(solution)/shard_map/ppermute | solution.py:24
  74.0 52.7 %collective-permute-start.3 = (f32[3,1,770,128]{3,2,1,0:T(8,128)S(1)}, f32[3,1,770,128]{3,2,1,0:T(8,128)}, u32[]{:S(2)}, u32[]{:S(2)}) collective-permute-start(f32[3,1,770,128]{3,2,1,0:T(8,128)S(1)} %get-tuple-element.76), channel_id=1, source_target_pairs={{0,1},{1,2},{2,3},{3,0},{4,5},{5,6},{6,7},{7,4},{8,9},{9,10},{10,1... | collective-permute-start | bytes 3548168 | tf_op jit(solution)/shard_map/ppermute | solution.py:21
  76.3 116.5 %copy-start.4 = (f32[128]{0:T(128)}, f32[128]{0:T(128)S(1)}, u32[]{:S(2)}) copy-start(f32[128]{0:T(128)S(1)} %get-tuple-element.94) | copy-start | bytes 1540
  93.6 33.0 %slice-start.9 = ((s8[9437184]{0:T(1024)(128)(4,1)}), s8[1048576]{0:T(1024)(128)(4,1)S(1)}, s32[]{:S(2)}) async-start(s8[9437184]{0:T(1024)(128)(4,1)} %bitcast.35), calls=%async_computation.11 | async-start | bytes 2097152
  234.3 4.8 collective-permute-start.6
  235.8 4.2 collective-permute-start.7
  309.1 238.1 %collective-permute-start.8 = (f32[15,1,770,128]{3,2,1,0:T(8,128)}, f32[15,1,770,128]{3,2,1,0:T(8,128)}, u32[]{:S(2)}, u32[]{:S(2)}) collective-permute-start(f32[15,1,770,128]{3,2,1,0:T(8,128)} %copy.105), channel_id=1, source_target_pairs={{0,1},{1,2},{2,3},{3,0},{4,5},{5,6},{6,7},{7,4},{8,9},{9,10},{10,1... | collective-permute-start | bytes 17740808 | tf_op jit(solution)/shard_map/ppermute | solution.py:21
  313.7 254.5 %collective-permute-start.9 = (f32[15,1,770,128]{3,2,1,0:T(8,128)}, f32[15,1,770,128]{3,2,1,0:T(8,128)}, u32[]{:S(2)}, u32[]{:S(2)}) collective-permute-start(f32[15,1,770,128]{3,2,1,0:T(8,128)} %copy.107), channel_id=1, source_target_pairs={{1,0},{2,1},{3,2},{0,3},{5,4},{6,5},{7,6},{4,7},{9,8},{10,9},{11,1... | collective-permute-start | bytes 17740808 | tf_op jit(solution)/shard_map/ppermute | solution.py:24
  320.3 109.7 %all-to-all-start = ((f32[3,8,768,128]{3,2,0,1:T(8,128)}), f32[3,8,768,128]{3,2,0,1:T(8,128)}, u32[]{:S(2)}, u32[]{:S(2)}) async-start(f32[3,8,768,128]{3,2,0,1:T(8,128)} %copy.80), calls=%async_computation | async-start | bytes 18874368 | tf_op jit(solution)/shard_map/all_to_all | solution.py:133
  539.8 455.6 %all-to-all-start.1 = ((f32[3,4,1536,128]{3,1,0,2:T(4,128)}), f32[3,4,1536,128]{3,1,0,2:T(4,128)}, u32[]{:S(2)}, u32[]{:S(2)}) async-start(f32[3,4,1536,128]{3,1,0,2:T(4,128)} %copy.82), calls=%async_computation.1 | async-start | bytes 18874368 | tf_op jit(solution)/shard_map/all_to_all | solution.py:140
  725.0 30.8 %collective-permute-start.10 = (f32[3,8,1,128]{3,1,2,0:T(8,128)S(1)}, f32[3,8,1,128]{3,1,2,0:T(8,128)S(1)}, u32[]{:S(2)}, u32[]{:S(2)}) collective-permute-start(f32[3,8,1,128]{3,1,2,0:T(8,128)S(1)} %get-tuple-element.65), channel_id=1, source_target_pairs={{0,16},{16,0},{1,17},{17,1},{2,18},{18,2},{3,19},{19,3},{4,20},{20... | collective-permute-start | bytes 36872 | tf_op jit(solution)/shard_map/ppermute | solution.py:21
  725.2 30.7 %collective-permute-start.11 = (f32[3,8,1,128]{3,1,2,0:T(8,128)S(1)}, f32[3,8,1,128]{3,1,2,0:T(8,128)S(1)}, u32[]{:S(2)}, u32[]{:S(2)}) collective-permute-start(f32[3,8,1,128]{3,1,2,0:T(8,128)S(1)} %get-tuple-element.66), channel_id=1, source_target_pairs={{16,0},{0,16},{17,1},{1,17},{18,2},{2,18},{19,3},{3,19},{20,4},{4,... | collective-permute-start | bytes 36872 | tf_op jit(solution)/shard_map/ppermute | solution.py:24
  745.1 30.2 %collective-permute-start.14 = (f32[3,8,768,1]{2,1,3,0:T(8,128)S(1)}, f32[3,8,768,1]{2,1,3,0:T(8,128)S(1)}, u32[]{:S(2)}, u32[]{:S(2)}) collective-permute-start(f32[3,8,768,1]{2,1,3,0:T(8,128)S(1)} %copy.113), channel_id=1, source_target_pairs={{4,0},{8,4},{12,8},{5,1},{9,5},{13,9},{6,2},{10,6},{14,10},{7,3},{... | collective-permute-start | bytes 221192 | tf_op jit(solution)/shard_map/ppermute | solution.py:24
  752.8 28.2 %collective-permute-start.15 = (f32[3,8,768,1]{2,1,3,0:T(8,128)S(1)}, f32[3,8,768,1]{2,1,3,0:T(8,128)S(1)}, u32[]{:S(2)}, u32[]{:S(2)}) collective-permute-start(f32[3,8,768,1]{2,1,3,0:T(8,128)S(1)} %copy.115), channel_id=1, source_target_pairs={{0,4},{4,8},{8,12},{1,5},{5,9},{9,13},{2,6},{6,10},{10,14},{3,7},{... | collective-permute-start | bytes 221192 | tf_op jit(solution)/shard_map/ppermute | solution.py:21
  764.5 54.4 %collective-permute-start.12 = (f32[3,1,770,128]{3,2,1,0:T(8,128)S(1)}, f32[3,1,770,128]{3,2,1,0:T(8,128)S(1)}, u32[]{:S(2)}, u32[]{:S(2)}) collective-permute-start(f32[3,1,770,128]{3,2,1,0:T(8,128)S(1)} %copy.109), channel_id=1, source_target_pairs={{1,0},{2,1},{3,2},{0,3},{5,4},{6,5},{7,6},{4,7},{9,8},{10,9},{11,1... | collective-permute-start | bytes 3548168 | tf_op jit(solution)/shard_map/ppermute | solution.py:24
  767.2 52.9 %collective-permute-start.13 = (f32[3,1,770,128]{3,2,1,0:T(8,128)}, f32[3,1,770,128]{3,2,1,0:T(8,128)}, u32[]{:S(2)}, u32[]{:S(2)}) collective-permute-start(f32[3,1,770,128]{3,2,1,0:T(8,128)} %copy.111), channel_id=1, source_target_pairs={{0,1},{1,2},{2,3},{3,0},{4,5},{5,6},{6,7},{7,4},{8,9},{9,10},{10,1... | collective-permute-start | bytes 3548168 | tf_op jit(solution)/shard_map/ppermute | solution.py:21
  781.0 41.6 %slice-start.15 = ((s8[9437184]{0:T(1024)(128)(4,1)}), s8[1048576]{0:T(1024)(128)(4,1)S(1)}, s32[]{:S(2)}) async-start(s8[9437184]{0:T(1024)(128)(4,1)} %bitcast.39), calls=%async_computation.17 | async-start | bytes 2097152
  786.7 36.0 %slice-start.16 = ((s8[9437184]{0:T(1024)(128)(4,1)}), s8[4194304]{0:T(1024)(128)(4,1)S(1)}, s32[]{:S(2)}) async-start(s8[9437184]{0:T(1024)(128)(4,1)} %bitcast.39), calls=%async_computation.18 | async-start | bytes 8388608
  786.7 36.0 %slice-start.17 = ((s8[9437184]{0:T(1024)(128)(4,1)}), s8[4194304]{0:T(1024)(128)(4,1)S(1)}, s32[]{:S(2)}) async-start(s8[9437184]{0:T(1024)(128)(4,1)} %bitcast.39), calls=%async_computation.19 | async-start | bytes 8388608
  786.7 36.0 %copy-start.7 = (f32[128]{0:T(128)S(1)}, f32[128]{0:T(128)}, u32[]{:S(2)}) copy-start(f32[128]{0:T(128)} %copy-done.6) | copy-start | bytes 1540
  (25 other events, 340.1 us)
where the time goes:
time: 1010 us; the launch traced here: 1000 us
  other arithmetic  446 us (44%)
  local copies, waits for them, and re-layouts  284 us (28%)
  waiting for transfers between devices  142 us (14%)
  matrix products  69.7 us (7%)
  starting transfers between devices  41.7 us (4%)
  blocking collectives  18.4 us (2%)
    all_to_all x1, waiting for transfers between devices, azimuth_filter(): lax.all_to_all(block_rows, 'az', split_axis=1, concat_axis=2, tiled=True)  102 us
    unnamed x76, local copies, waits for them, and re-layouts  73.4 us
    add x1, other arithmetic, smooth(): 0.25 * source[:, :-2] + 0.5 * source[:, 1:-1] + 0.25 * source[:, 2:]  65.1 us
    unnamed x21, other arithmetic  62.1 us
    add x1, other arithmetic, smooth(): 0.25 * partial_value[:, :, :-2] + 0.5 * partial_value[:, :, 1:-1]  59.7 us
    slice x6, local copies, waits for them, and re-layouts, extended(): lax.slice_in_dim(block, block.shape[dim] - width, None, axis=dim)  41.6 us
    concatenate x2, other arithmetic, extended(): block = jnp.concatenate([low, block, high], axis=dim)  39.1 us
    mul x2, other arithmetic, identity_sums(): 2.0 * scale_sq * (hat_model - 4.0 * hat_magnitude * hat_tensor)  37.9 us
  transfers between devices with their start and end apart: 18, of which 6 were waited for; matrix products, arithmetic and copies ran while one was open for 60% of the time, Pallas kernels for 0%

commit v1 on v0

v1 whole, which is shorter than its diff:
```python
import functools
import math

import jax
import jax.numpy as jnp
import numpy as np
from jax import lax
from jax.experimental import pallas as pl
from jax.experimental.pallas import tpu as pltpu
from jax.sharding import PartitionSpec as P

MODES = 512
NODES = 48
PAD = 16
CHUNK = 16
F32 = jnp.float32
BF16 = jnp.bfloat16
PAIRS = ((0, 0), (1, 1), (2, 2), (0, 1), (0, 2), (1, 2))


def shift_from(block, axis, step, periodic=True):
    count = lax.axis_size(axis)
    pairs = [((i + step) % count, i) for i in range(count) if periodic or 0 <= i + step < count]
    return lax.ppermute(block, axis, pairs)


def spacing_of(shell_pos, azimuths):
    return jnp.maximum(shell_pos * (2.0 * math.pi / azimuths), 1.0)


def stencil_kernel(rows, below_ref, here_ref, above_ref, edge_ref, lane_ref,
                   mag_ref, sums_ref, prev_q, prev_h, full):
    step = pl.program_id(0)
    inv_pos = lane_ref[0:1, :]
    half_space = lane_ref[1:2, :]
    scale = lane_ref[2:3, :]
    lane = lax.broadcasted_iota(jnp.int32, (CHUNK, 128), 1)

    @pl.when(step == 0)
    def _():
        prev_q[...] = jnp.zeros_like(prev_q)
        prev_h[...] = jnp.zeros_like(prev_h)
        sums_ref[...] = jnp.zeros_like(sums_ref)

    def produce(i, carry):
        base = pl.multiple_of(i * CHUNK, 8)
        here = pl.ds(base + 8, CHUNK)
        out = pl.ds(base, CHUNK)
        v, dz, dt, dr = [], [], [], []
        for c in range(3):
            wide = here_ref[c, 0, pl.ds(base, CHUNK + 16), :]
            mid = wide[8 : 8 + CHUNK]
            edge = edge_ref[c, 0, here, :]
            v.append(mid)
            dt.append((wide[9 : 9 + CHUNK] - wide[7 : 7 + CHUNK]) * half_space)
            dz.append((above_ref[c, 0, here, :] - below_ref[c, 0, here, :]) * 0.5)
            up = jnp.where(lane == 127, edge, pltpu.roll(mid, 127, 1))
            down = jnp.where(lane == 0, edge, pltpu.roll(mid, 1, 1))
            dr.append((up - down) * 0.5)
        tensor = [
            dz[0],
            dr[1],
            dt[2] + v[1] * inv_pos,
            0.5 * (dr[0] + dz[1]),
            0.5 * (dt[0] + dz[2]),
            0.5 * (dr[2] - v[2] * inv_pos + dt[1]),
        ]
        diag = tensor[0] * tensor[0] + tensor[1] * tensor[1] + tensor[2] * tensor[2]
        off = tensor[3] * tensor[3] + tensor[4] * tensor[4] + tensor[5] * tensor[5]
        mag = jnp.sqrt(2.0 * diag + 4.0 * off)
        mag_ref[0, out, :] = mag
        fields = v + [v[a] * v[b] for a, b in PAIRS] + tensor + [mag * x for x in tensor]
        for f, q in enumerate(fields):
            h = prev_q[f, out, :] + q
            full[f, out, :] = prev_h[f, out, :] + h
            prev_q[f, out, :] = q
            prev_h[f, out, :] = h
        return carry

    lax.fori_loop(0, (rows + 16) // CHUNK, produce, 0)

    def smoothed(f, base):
        wide = full[f, pl.ds(base, CHUNK + 16), :]
        mid = wide[8 : 8 + CHUNK]
        return (wide[7 : 7 + CHUNK] + wide[9 : 9 + CHUNK] + (mid + mid)) * 0.0625

    def consume(i, carry):
        num, den = carry
        base = pl.multiple_of(i * CHUNK, 8)
        hat_v = [smoothed(c, base) for c in range(3)]
        leo = [smoothed(3 + n, base) - hat_v[a] * hat_v[b] for n, (a, b) in enumerate(PAIRS)]
        third = (leo[0] + leo[1] + leo[2]) * (1.0 / 3.0)
        leo = [x - third for x in leo[:3]] + leo[3:]
        hat_t = [smoothed(9 + n, base) for n in range(6)]
        diag = hat_t[0] * hat_t[0] + hat_t[1] * hat_t[1] + hat_t[2] * hat_t[2]
        off = hat_t[3] * hat_t[3] + hat_t[4] * hat_t[4] + hat_t[5] * hat_t[5]
        four_mag = 4.0 * jnp.sqrt(2.0 * diag + 4.0 * off)
        lm_d = lm_o = mm_d = mm_o = 0.0
        for n in range(6):
            model = (smoothed(15 + n, base) - four_mag * hat_t[n]) * scale
            lm, mm = leo[n] * model, model * model
            if n < 3:
                lm_d, mm_d = lm_d + lm, mm_d + mm
            else:
                lm_o, mm_o = lm_o + lm, mm_o + mm
        return (num + (lm_d + 2.0 * lm_o), den + (mm_d + 2.0 * mm_o))

    @pl.when(step >= 2)
    def _():
        zero = jnp.zeros((CHUNK, 128), F32)
        num, den = lax.fori_loop(0, rows // CHUNK, consume, (zero, zero))
        sums_ref[0] += num
        sums_ref[1] += den


def stencil(padded, edges, lanes):
    _, deep, tall, width = padded.shape
    rows = tall - 2 * PAD
    steps = deep - 2
    block = (3, 1, tall, width)
    return pl.pallas_call(
        functools.partial(stencil_kernel, rows),
        grid=(steps,),
        in_specs=[
            pl.BlockSpec(block, lambda j: (0, j, 0, 0)),
            pl.BlockSpec(block, lambda j: (0, j + 1, 0, 0)),
            pl.BlockSpec(block, lambda j: (0, j + 2, 0, 0)),
            pl.BlockSpec(block, lambda j: (0, j, 0, 0)),
            pl.BlockSpec((8, width), lambda j: (0, 0)),
        ],
        out_specs=[
            pl.BlockSpec((1, rows + 16, width), lambda j: (j, 0, 0)),
            pl.BlockSpec((2, CHUNK, width), lambda j: (0, 0, 0)),
        ],
        out_shape=[
            jax.ShapeDtypeStruct((steps, rows + 16, width), F32),
            jax.ShapeDtypeStruct((2, CHUNK, width), F32),
        ],
        scratch_shapes=[pltpu.VMEM((21, rows + 16, width), F32)] * 3,
        compiler_params=pltpu.CompilerParams(vmem_limit_bytes=58 * 2**20),
        cost_estimate=pl.CostEstimate(flops=10**9, bytes_accessed=10**8, transcendentals=0),
        name="stencil",
    )(padded, padded, padded, edges, lanes)


def split(x):
    high = x.astype(BF16)
    return high, (x - high.astype(F32)).astype(BF16)


def split_table(x):
    high = lax.reduce_precision(x, 8, 7)
    return high.astype(BF16), (x - high).astype(BF16)


def mm(a, b):
    return jnp.dot(a, b, preferred_element_type=F32)


def cross_tables(azimuths, parts):
    local = azimuths // parts
    pos = math.pi * (np.arange(local) - (local - 1) / 2.0) / azimuths
    edge = math.tan(math.pi * local / (2.0 * azimuths)) if parts > 1 else 1.0
    ratio = np.tan(pos) / edge
    var = np.log((1.0 + ratio) / (1.0 - ratio))
    reach = var[-1]
    theta = (np.arange(NODES) + 0.5) * math.pi / NODES
    nodes = reach * np.cos(theta)
    node_pos = np.arctan(edge * np.tanh(nodes / 2.0))
    weight = np.sin(theta) * (-1.0) ** np.arange(NODES)
    gap = var[:, None] - nodes[None, :]
    gap = np.where(np.abs(gap) < 1e-13, 1e-13, gap)
    lag = weight[None, :] / gap
    lag = lag / np.sum(lag, axis=1, keepdims=True)
    spread = lag / np.cos(pos)[:, None]
    gather = []
    for away in range(1, parts):
        source = pos + math.pi * local * away / azimuths
        gather.append(np.cos(node_pos)[:, None] / np.sin(node_pos[:, None] - source[None, :]) / azimuths)
    return spread.astype(np.float32), np.stack(gather).astype(np.float32)


def twice(x):
    return jnp.concatenate([x, x], axis=1)


def moment_kernel(x_ref, wave_ref, turn_ref, table_ref, out_ref):
    x = jnp.concatenate([x_ref[0, 0], x_ref[0, 1]], axis=1)
    c_hi, c_lo = split(x * twice(wave_ref[0]))
    s_hi, s_lo = split(x * twice(wave_ref[1]))
    for away in range(table_ref.shape[0]):
        table = table_ref[away]

        def apply(high, low):
            both = mm(table, high)
            return both[:NODES] + (both[NODES:] + mm(table[:NODES], low))

        by_cos, by_sin = apply(c_hi, c_lo), apply(s_hi, s_lo)
        cos_turn = twice(turn_ref[away, 0:1])
        sin_turn = twice(turn_ref[away, 1:2])
        first = by_cos * cos_turn - by_sin * sin_turn
        second = by_sin * cos_turn + by_cos * sin_turn
        for k in range(2):
            cols = slice(128 * k, 128 * k + 128)
            out_ref[away, 0, k, :NODES] = first[:, cols]
            out_ref[away, 0, k, NODES:] = second[:, cols]


def filter_kernel(x_ref, far_ref, live_ref, scaling_ref, wave_ref, spread_ref,
                  fwd_hi, fwd_lo, inv_hi, inv_lo, out_ref):
    x = jnp.concatenate([x_ref[0, 0], x_ref[0, 1]], axis=1)
    x_hi, x_lo = split(x)
    spectrum = mm(fwd_hi[...], x_hi) + (mm(fwd_hi[...], x_lo) + mm(fwd_lo[...], x_hi))
    s_hi, s_lo = split(spectrum * twice(scaling_ref[...]))
    near = mm(inv_hi[...], s_hi) + (mm(inv_hi[...], s_lo) + mm(inv_lo[...], s_hi))
    far = jnp.concatenate([far_ref[0, 0], far_ref[0, 1]], axis=1)
    f_hi, f_lo = split(far)

    def spread(rows):
        stacked = jnp.concatenate([f_hi[rows], f_lo[rows], f_hi[rows]], axis=0)
        return mm(spread_ref[...], stacked)

    by_cos = spread(slice(0, NODES))
    by_sin = spread(slice(NODES, 2 * NODES))
    result = near + (twice(wave_ref[1]) * by_cos - twice(wave_ref[0]) * by_sin)
    result = jnp.where(twice(live_ref[0]) > 0.5, result, x)
    out_ref[0, 0] = result[:, :128]
    out_ref[0, 1] = result[:, 128:]


def polar_tables(cutoffs, columns, azimuths):
    order = 2 * cutoffs + 1
    offset = 2 * jnp.arange(columns, dtype=jnp.int32) - (columns - 1)
    unit = math.pi / (2.0 * azimuths)
    phase = (offset[:, None] * order[None, :] % (4 * azimuths)).astype(F32) * unit
    wave = jnp.stack([jnp.cos(phase), jnp.sin(phase)])
    modes = jnp.arange(MODES, dtype=jnp.int32)
    angle = (2 * offset[None, :] * modes[:, None] % (4 * azimuths)).astype(F32) * unit
    fourier = jnp.concatenate([jnp.cos(angle), jnp.sin(angle)], axis=0)
    weight = jnp.where(modes == 0, 1.0, 2.0).astype(F32) / azimuths
    kept = jnp.where(modes[:, None] <= cutoffs[None, :], weight[:, None], 0.0)
    return wave, fourier, jnp.concatenate([kept, kept], axis=0)


def moments(velocity, wave, turn, table):
    comps, planes, columns, width = velocity.shape
    far = table.shape[0]
    return pl.pallas_call(
        moment_kernel,
        grid=(comps, planes // 2),
        in_specs=[
            pl.BlockSpec((1, 2, columns, width), lambda c, z: (c, z, 0, 0)),
            pl.BlockSpec(wave.shape, lambda c, z: (0, 0, 0)),
            pl.BlockSpec(turn.shape, lambda c, z: (0, 0, 0)),
            pl.BlockSpec(table.shape, lambda c, z: (0, 0, 0)),
        ],
        out_specs=pl.BlockSpec((far, 1, 2, 2 * NODES, width), lambda c, z: (0, c, z, 0, 0)),
        out_shape=jax.ShapeDtypeStruct((far, comps, planes, 2 * NODES, width), F32),
        name="moments",
    )(velocity, wave, turn, table)


def filtered_of(velocity, far, live, scaling, wave, spread, fourier):
    comps, planes, columns, width = velocity.shape
    fwd_hi, fwd_lo = split_table(fourier)
    tables = (fwd_hi, fwd_lo, fwd_hi.T, fwd_lo.T)

    def whole(x):
        return pl.BlockSpec(x.shape, lambda c, z: (0,) * x.ndim, pipeline_mode=pl.Buffered(1))

    block = pl.BlockSpec((1, 2, columns, width), lambda c, z: (c, z, 0, 0))
    return pl.pallas_call(
        filter_kernel,
        grid=(comps, planes // 2),
        in_specs=[
            block,
            pl.BlockSpec((1, 2, 2 * NODES, width), lambda c, z: (c, z, 0, 0)),
            pl.BlockSpec((1, 1, width), lambda c, z: (c, 0, 0)),
            whole(scaling), whole(wave), whole(spread),
        ] + [whole(t) for t in tables],
        out_specs=block,
        out_shape=jax.ShapeDtypeStruct(velocity.shape, F32),
        compiler_params=pltpu.CompilerParams(vmem_limit_bytes=58 * 2**20),
        cost_estimate=pl.CostEstimate(flops=30 * 10**9, bytes_accessed=2 * 10**7, transcendentals=0),
        name="polar",
    )(velocity, far, live, scaling, wave, spread, *tables)


def polar_step(velocity, cutoff, shells, first_shell):
    comps, planes, columns, width = velocity.shape
    parts = lax.axis_size("az")
    azimuths = columns * parts
    inner_side = lax.axis_index("rad") < lax.axis_size("rad") // 2
    cutoffs = lax.dynamic_slice_in_dim(cutoff, first_shell, width)
    shell_ids = first_shell + jnp.arange(width, dtype=jnp.int32)
    live = (shell_ids[None, None, :] < shells[:, None, None]).astype(F32)
    spread, gather = cross_tables(azimuths, parts)
    g_hi, g_lo = split_table(jnp.asarray(gather))
    table = jnp.concatenate([g_hi, g_lo], axis=1)
    s_hi, s_lo = split_table(jnp.asarray(spread))
    spread_table = jnp.concatenate([s_hi, s_hi, s_lo], axis=1)
    away = jnp.arange(1, parts, dtype=jnp.int32)
    turned = (away[:, None] * (2 * cutoffs[None, :] + 1) % (2 * parts)).astype(F32) * (math.pi / parts)
    turn = jnp.stack([jnp.cos(turned), jnp.sin(turned)], axis=1)
    far_shape = (parts - 1, comps, planes, 2 * NODES, width)

    def gather_far(v):
        wave, _, _ = polar_tables(cutoffs, columns, azimuths)
        return moments(v, wave, turn, table)

    sent = lax.cond(inner_side, gather_far, lambda v: jnp.zeros(far_shape, F32), velocity)
    far = shift_from(sent[0], "az", 1)
    for n in range(1, parts - 1):
        far = far + shift_from(sent[n], "az", n + 1)

    def apply(v, f):
        wave, fourier, scaling = polar_tables(cutoffs, columns, azimuths)
        return filtered_of(v, f, live, scaling, wave, spread_table, fourier)

    return lax.cond(inner_side, apply, lambda v, f: v, velocity, far)


def local(velocity, cutoff, shells):
    _, planes, columns, radial = velocity.shape
    azimuths = columns * lax.axis_size("az")
    surface_cells = planes * lax.axis_size("ax") * azimuths
    first_shell = lax.axis_index("rad") * radial
    shell_pos = first_shell.astype(F32) + jnp.arange(radial, dtype=F32) + 0.5
    spacing = spacing_of(shell_pos, azimuths)
    scale_sq = jnp.power(spacing, 2.0 / 3.0)

    filtered = polar_step(velocity, cutoff, shells, first_shell)

    low_z = shift_from(velocity[:, -2:], "ax", -1)
    high_z = shift_from(velocity[:, :2], "ax", 1)
    tall = jnp.concatenate([low_z, velocity, high_z], axis=1)
    low_t = shift_from(tall[:, :, -PAD:], "az", -1)
    high_t = shift_from(tall[:, :, :PAD], "az", 1)
    padded = jnp.concatenate([low_t, tall, high_t], axis=2)
    inside = padded[:, 1:-1]
    lower = shift_from(inside[..., -1], "rad", -1, False)[..., None]
    upper = shift_from(inside[..., 0], "rad", 1, False)[..., None]
    lane = jnp.arange(radial)
    edges = jnp.where(lane == 0, lower, jnp.where(lane == radial - 1, upper, 0.0))
    lanes = jnp.zeros((8, radial), F32)
    lanes = lanes.at[0].set(1.0 / shell_pos).at[1].set(0.5 / spacing).at[2].set(2.0 * scale_sq)
    magnitude, sums = stencil(padded, edges, lanes)

    totals = lax.psum(jnp.sum(sums, axis=1), ("az", "ax"))
    coefficient = totals[0] / surface_cells / (totals[1] / surface_cells + 1e-06)
    viscosity = coefficient * scale_sq * magnitude[1:-1, 8:-8]
    return (filtered, viscosity, coefficient)


def solution(mesh):
    in_specs = (P(None, "ax", "az", "rad"), P(), P())
    out_specs = (P(None, "ax", "az", "rad"), P("ax", "az", "rad"), P("rad"))
    return jax.shard_map(local, mesh=mesh, in_specs=in_specs, out_specs=out_specs, check_vma=False)
```

time: 1010 us -> 382 us (0.38)
  other arithmetic: 446 us -> 33.8 us
  local copies, waits for them, and re-layouts: 284 us -> 47.5 us
  Pallas kernels: 0 us -> 173 us
  matrix products: 69.7 us -> 0 us
  waiting for transfers between devices: 142 us -> 91.7 us
  starting transfers between devices: 41.7 us -> 12.2 us
    pallas_call x0 -> x3, Pallas kernels: none -> 173 us  [the longest x1 96.1 us: stencil(): pl.pallas_call(functools.partial(stencil_kernel, rows), grid=(steps,), in...]
    add x4 -> x3, other arithmetic: 125 us -> 0.01 us  [the longest x2 0.01 us: polar_tables(): order = 2 * cutoffs + 1]
    mul x10 -> x4, other arithmetic: 123 us -> 4.32 us  [the longest x2 4.29 us: local(): viscosity = coefficient * scale_sq * magnitude[1:-1, 8:-8]]
    all_to_all x2 -> x0, waiting for transfers between devices: 102 us -> none  [the longest x1 102 us: azimuth_filter(): lax.all_to_all(block_rows, 'az', split_axis=1, concat_axis=2, tiled=True)]
    slice x18 -> x5, local copies, waits for them, and re-layouts: 128 us -> 33.4 us  [the longest x2 19.6 us: local(): lower = shift_from(inside[..., -1], 'rad', -1, False)[..., None]]
    dot_general x2 -> x0, matrix products: 69.7 us -> none  [the longest x1 35.4 us: polar_filter(): jnp.einsum('czmr,tm->cztr', spectrum * scaling[:, None], fourier, precisi...]
    unnamed x76 -> x10, local copies, waits for them, and re-layouts: 73.4 us -> 8.17 us
    unnamed x21 -> x0, other arithmetic: 62.1 us -> none
  transfers between devices with their start and end apart: 18 -> 7, of which waited for: 6 -> 4; matrix products, arithmetic and copies ran while one was open for 60% -> 16% of each run, Pallas kernels for 0% -> 20%
where the time goes in v1:
time: 382 us; the launch traced here: 381 us
  Pallas kernels  173 us (45%)
  waiting for transfers between devices  91.7 us (24%)
  local copies, waits for them, and re-layouts  47.5 us (12%)
  other arithmetic  33.8 us (9%)
  blocking collectives  22 us (6%)
  starting transfers between devices  12.2 us (3%)
    pallas_call x1, Pallas kernels, stencil(): pl.pallas_call(functools.partial(stencil_kernel, rows), grid=(steps,), in...  96.1 us
    ppermute x7, waiting for transfers between devices, shift_from(): return lax.ppermute(block, axis, pairs)  91.7 us
    pallas_call x1, Pallas kernels, filtered_of(): pl.pallas_call(filter_kernel, grid=(comps, planes // 2), in_specs=[block,...  66.5 us
    psum x1, blocking collectives, local(): totals = lax.psum(jnp.sum(sums, axis=1), ('az', 'ax'))  22 us
    slice x2, local copies, waits for them, and re-layouts, local(): lower = shift_from(inside[..., -1], 'rad', -1, False)[..., None]  19.6 us
    ppermute x7, starting transfers between devices, shift_from(): return lax.ppermute(block, axis, pairs)  12.2 us
    pallas_call x1, Pallas kernels, moments(): pl.pallas_call(moment_kernel, grid=(comps, planes // 2), in_specs=[pl.Blo...  10.6 us
    slice x1, local copies, waits for them, and re-layouts, local(): upper = shift_from(inside[..., 0], 'rad', 1, False)[..., None]  8.94 us
  transfers between devices with their start and end apart: 7, of which 4 were waited for; matrix products, arithmetic and copies ran while one was open for 16% of the time, Pallas kernels for 20%

profile of v1, /device:TPU:0, one launch (start us, length us, event | category | flops | bytes accessed | tf_op | source)
XLA Modules:
  0.0 381.5 jit_solution(7387678096461166483)
XLA Ops:
  0.6 4.9 %fusion.32 = (f32[3,2,768,128]{3,2,1,0:T(8,128)}, f32[3,2,768,128]{3,2,1,0:T(8,128)}) fusion(f32[3,8,768,128]{3,2,1,0:T(8,128)} %param.15), kind=kLoop, calls=%fused_computation.72 | loop fusion | bytes 9437184 | tf_op jit(solution)/shard_map/slice | solution.py:335
  5.5 3.1 collective-permute-start.1
  8.5 2.0 collective-permute-start.2
  11.4 13.3 %conditional.2 = (f32[1,3,8,96,128]{4,3,2,1,0:T(8,128)S(1)}) conditional(s32[]{:T(128)} %convert_element_type.73, () %tuple.32, (s32[128]{0:T(128)S(1)}, f32[3,8,768,128]{3,2,1,0:T(8,128)}, f32[1,2,128]{2,1,0:T(2,128)S(1)}) %tuple.38), branch_computations={%region_0.1_spmd, %region_1.2_spmd.clone} | conditional | flops 1083136 | bytes 2366984 | solution.py:311
  14.1 10.6 %moments.1 = f32[1,3,8,96,128]{4,3,2,1,0:T(8,128)S(1)} custom-call(f32[3,8,768,128]{3,2,1,0:T(8,128)} %get-tuple-element.77.x_ref, f32[2,768,128]{2,1,0:T(8,128)} %pad_maximum_fusion.wave_ref, f32[1,2,128]{2,1,0:T(2,128)S(1)} %get-tuple-element.79.turn_ref, bf16[1,96,768]{2,1,0:T(8,128)(2,1)} %constant.215.table_ref), custom_call_target="tpu_custom_call" | custom-call | tf_op jit(solution)/shard_map/cond/branch_1_fun/moments/pallas_call | solution.py:248
  26.6 36.4 %collective-permute-done.1 = f32[3,2,768,128]{3,2,1,0:T(8,128)} collective-permute-done((f32[3,2,768,128]{3,2,1,0:T(8,128)}, f32[3,2,768,128]{3,2,1,0:T(8,128)}, u32[]{:S(2)}, u32[]{:S(2)}) %collective-permute-start.1) | collective-permute-done | bytes 2359328 | tf_op jit(solution)/shard_map/ppermute | solution.py:24
  64.9 4.4 %constant_dynamic-update-slice_fusion.1 = f32[3,12,768,128]{3,2,1,0:T(8,128)S(1)} fusion(f32[3,12,768,128]{3,2,1,0:T(8,128)S(1)} %constant_dynamic-update-slice_fusion.2, f32[3,8,768,128]{3,2,1,0:T(8,128)} %param.15), kind=kLoop, calls=%fused_computation.47 | loop fusion | bytes 18874368
  69.3 42.7 %collective-permute-done.2 = f32[3,2,768,128]{3,2,1,0:T(8,128)S(1)} collective-permute-done((f32[3,2,768,128]{3,2,1,0:T(8,128)}, f32[3,2,768,128]{3,2,1,0:T(8,128)S(1)}, u32[]{:S(2)}, u32[]{:S(2)}) %collective-permute-start.2) | collective-permute-done | bytes 2359328 | tf_op jit(solution)/shard_map/ppermute | solution.py:24
  114.4 7.8 %collective-permute-done.3 = f32[3,12,16,128]{3,2,1,0:T(8,128)S(1)} collective-permute-done((f32[3,12,16,128]{3,2,1,0:T(8,128)S(1)}, f32[3,12,16,128]{3,2,1,0:T(8,128)S(1)}, u32[]{:S(2)}, u32[]{:S(2)}) %collective-permute-start.3) | collective-permute-done | bytes 294944 | tf_op jit(solution)/shard_map/ppermute | solution.py:24
  122.2 4.8 %collective-permute-done.4 = f32[3,12,16,128]{3,2,1,0:T(8,128)S(1)} collective-permute-done((f32[3,12,16,128]{3,2,1,0:T(8,128)S(1)}, f32[3,12,16,128]{3,2,1,0:T(8,128)S(1)}, u32[]{:S(2)}, u32[]{:S(2)}) %collective-permute-start.4) | collective-permute-done | bytes 294944 | tf_op jit(solution)/shard_map/ppermute | solution.py:24
  127.0 5.9 %pad_maximum_fusion.4.below_ref.here_ref.above_ref = f32[3,12,800,128]{3,2,1,0:T(8,128)S(1)} fusion(f32[3,12,16,128]{3,2,1,0:T(8,128)S(1)} %collective-permute-done.4, f32[3,12,768,128]{3,2,1,0:T(8,128)} %copy-done.1, f32[3,12,16,128]{3,2,1,0:T(8,128)S(1)} %collective-permute-done.3), kind=kLoop, calls=%fused_computation.43 | loop fusion | flops 7372800 | bytes 29491200 | tf_op jit(solution)/shard_map/concatenate | solution.py:339
  132.9 10.6 %fusion.30 = (f32[3,10,800,1]{3,2,1,0:T(8,128)}, f32[3,10,800,1]{3,2,1,0:T(8,128)}) fusion(f32[3,12,800,128]{3,2,1,0:T(8,128)S(1)} %pad_maximum_fusion.4.below_ref.here_ref.above_ref), kind=kLoop, calls=%fused_computation.70 | loop fusion | bytes 384000 | tf_op jit(solution)/shard_map/slice | solution.py:341
  143.6 1.9 copy-done
  145.5 8.9 %copy.12 = f32[3,10,800,1]{2,0,1,3:T(4,128)} copy(f32[3,10,800,1]{3,2,1,0:T(8,128)} %get-tuple-element.104) | data formatting | bytes 192000 | tf_op jit(solution)/shard_map/slice | solution.py:341
  154.4 1.9 collective-permute-start.5
  156.4 8.9 %copy.14 = f32[3,10,800,1]{2,0,1,3:T(4,128)} copy(f32[3,10,800,1]{3,2,1,0:T(8,128)} %get-tuple-element.105) | data formatting | bytes 192000 | tf_op jit(solution)/shard_map/slice | solution.py:342
  166.6 81.2 %conditional.3 = (f32[3,8,768,128]{3,2,1,0:T(8,128)}) conditional(s32[]{:T(128)} %convert_element_type.73, f32[3,8,768,128]{3,2,1,0:T(8,128)} %param.15, (s32[128]{0:T(128)S(1)}, f32[3,8,768,128]{3,2,1,0:T(8,128)}, f32[3,8,96,128]{3,2,1,0:T(8,128)}, f32[3,1,128]{2,1,0:T(1,128)S(1)}) %tuple.39), branch_computations={%region_2.3_spmd, %region_3.4_spmd.clone} | conditional | flops 30008821760 | bytes 51737920 | solution.py:320
  166.9 6.4 %fusion.13 = (f32[512,768]{0,1:T(8,128)S(1)}, f32[512,768]{0,1:T(8,128)S(1)}) fusion(s32[768]{0:T(1024)S(1)} %broadcast_multiply_fusion), kind=kLoop, calls=%fused_computation.23 | loop fusion | flops 3538944 | bytes 3148800 | tf_op jit(solution)/shard_map/cond/branch_1_fun/cos | solution.py:239
  174.0 2.2 copy.16.fwd_hi
  181.3 66.5 %polar.1 = f32[3,8,768,128]{3,2,1,0:T(8,128)} custom-call(f32[3,8,768,128]{3,2,1,0:T(8,128)} %get-tuple-element.83.x_ref, f32[3,8,96,128]{3,2,1,0:T(8,128)} %get-tuple-element.84.far_ref, f32[3,1,128]{2,1,0:T(1,128)S(1)} %get-tuple-element.85.live_ref, f32[1024,128]{1,0:T(8,128)} %pad_maximum_fusion.3.scaling_ref, ...), custom_call_target="tpu_custom_call" | custom-call | flops 30000001024 | bytes 20000000 | tf_op jit(solution)/shard_map/cond/branch_1_fun/polar/pallas_call | solution.py:272
  249.7 8.6 %select_select_fusion.edge_ref = f32[3,10,800,128]{3,2,1,0:T(8,128)} fusion(f32[3,10,800]{2,1,0:T(8,128)S(1)} %copy.15, f32[3,10,800]{2,1,0:T(8,128)S(1)} %copy.13, pred[128]{0:T(512)(128)(4,1)S(1)} %get-tuple-element.110, pred[128]{0:T(512)(128)(4,1)S(1)} %get-tuple-element.111), kind=kLoop, calls=%fused_computation.44 | loop fusion | flops 6144000 | bytes 12480256 | tf_op jit(solution)/shard_map/jit(_where)/select_n | solution.py:344
  258.4 96.1 %stencil.1 = (f32[10,784,128]{2,1,0:T(8,128)}, f32[2,16,128]{2,1,0:T(8,128)}) custom-call(f32[3,12,800,128]{3,2,1,0:T(8,128)} %copy-done, f32[3,12,800,128]{3,2,1,0:T(8,128)} %copy-done, f32[3,12,800,128]{3,2,1,0:T(8,128)} %copy-done, f32[3,10,800,128]{3,2,1,0:T(8,128)} %select_select_fusion.edge_ref, f32[8,128]{1,0:T(8,128)} %copy-done.4), custom_call_target="tpu_custom_call" | custom-call | flops 1000000000 | bytes 100000000 | tf_op jit(solution)/shard_map/stencil/pallas_call | solution.py:121
  355.2 22.0 %psum.7 = f32[2,128]{1,0:T(2,128)S(1)} all-reduce(f32[2,128]{1,0:T(2,128)S(1)} %reduce_sum.9), channel_id=1, replica_groups=mesh['az'=2,'rad'=4,'ax'=4] {'az','ax'}, use_global_device_ids=true, to_apply=%region_5.6 | all-reduce | flops 256 | bytes 2048 | tf_op jit(solution)/shard_map/psum | solution.py:349
  377.7 3.8 slice_multiply_fusion
  (50 shorter events, 19.8 us)
Async XLA Ops:
  5.5 57.5 %collective-permute-start.1 = (f32[3,2,768,128]{3,2,1,0:T(8,128)}, f32[3,2,768,128]{3,2,1,0:T(8,128)}, u32[]{:S(2)}, u32[]{:S(2)}) collective-permute-start(f32[3,2,768,128]{3,2,1,0:T(8,128)} %get-tuple-element.109), channel_id=1, source_target_pairs={{3,0},{0,1},{1,2},{2,3},{7,4},{4,5},{5,6},{6,7},{11,8},{8,9},{9,10... | collective-permute-start | bytes 7077896 | tf_op jit(solution)/shard_map/ppermute | solution.py:24
  8.5 103.5 %collective-permute-start.2 = (f32[3,2,768,128]{3,2,1,0:T(8,128)}, f32[3,2,768,128]{3,2,1,0:T(8,128)S(1)}, u32[]{:S(2)}, u32[]{:S(2)}) collective-permute-start(f32[3,2,768,128]{3,2,1,0:T(8,128)} %get-tuple-element.108), channel_id=1, source_target_pairs={{1,0},{2,1},{3,2},{0,3},{5,4},{6,5},{7,6},{4,7},{9,8},{10,9},{11,1... | collective-permute-start | bytes 7077896 | tf_op jit(solution)/shard_map/ppermute | solution.py:24
  24.7 141.9 %collective-permute-start = (f32[3,8,96,128]{3,2,1,0:T(8,128)S(1)}, f32[3,8,96,128]{3,2,1,0:T(8,128)}, u32[]{:S(2)}, u32[]{:S(2)}) collective-permute-start(f32[3,8,96,128]{3,2,1,0:T(8,128)S(1)} %bitcast.16), channel_id=1, source_target_pairs={{16,0},{0,16},{17,1},{1,17},{18,2},{2,18},{19,3},{3,19},{20,4},{4,... | collective-permute-start | bytes 3538952 | tf_op jit(solution)/shard_map/ppermute | solution.py:24
  26.6 42.7 %copy-start.4 = (f32[8,128]{1,0:T(8,128)}, f32[8,128]{1,0:T(8,128)S(1)}, u32[]{:S(2)}) copy-start(f32[8,128]{1,0:T(8,128)S(1)} %scatter.14.lane_ref) | copy-start | bytes 12292
  69.3 45.1 %copy-start.5 = (s32[3]{0:T(128)S(1)}, s32[3]{0:T(128)}, u32[]{:S(2)}) copy-start(s32[3]{0:T(128)} %param.17) | copy-start | bytes 40
  112.2 10.0 %copy-start.1 = (f32[3,12,768,128]{3,2,1,0:T(8,128)}, f32[3,12,768,128]{3,2,1,0:T(8,128)S(1)}, u32[]{:S(2)}) copy-start(f32[3,12,768,128]{3,2,1,0:T(8,128)S(1)} %constant_dynamic-update-slice_fusion) | copy-start | bytes 42467332
  112.3 9.9 %collective-permute-start.3 = (f32[3,12,16,128]{3,2,1,0:T(8,128)S(1)}, f32[3,12,16,128]{3,2,1,0:T(8,128)S(1)}, u32[]{:S(2)}, u32[]{:S(2)}) collective-permute-start(f32[3,12,16,128]{3,2,1,0:T(8,128)S(1)} %get-tuple-element.106), channel_id=1, source_target_pairs={{16,0},{0,16},{17,1},{1,17},{18,2},{2,18},{19,3},{3,19},{20,4},{4,... | collective-permute-start | bytes 884744 | tf_op jit(solution)/shard_map/ppermute | solution.py:24
  113.8 13.2 %collective-permute-start.4 = (f32[3,12,16,128]{3,2,1,0:T(8,128)S(1)}, f32[3,12,16,128]{3,2,1,0:T(8,128)S(1)}, u32[]{:S(2)}, u32[]{:S(2)}) collective-permute-start(f32[3,12,16,128]{3,2,1,0:T(8,128)S(1)} %get-tuple-element.107), channel_id=1, source_target_pairs={{16,0},{0,16},{17,1},{1,17},{18,2},{2,18},{19,3},{3,19},{20,4},{4,... | collective-permute-start | bytes 884744 | tf_op jit(solution)/shard_map/ppermute | solution.py:24
  132.9 12.6 %copy-start = (f32[3,12,800,128]{3,2,1,0:T(8,128)}, f32[3,12,800,128]{3,2,1,0:T(8,128)S(1)}, u32[]{:S(2)}) copy-start(f32[3,12,800,128]{3,2,1,0:T(8,128)S(1)} %pad_maximum_fusion.4.below_ref.here_ref.above_ref) | copy-start | bytes 44236804
  154.4 93.4 %collective-permute-start.5 = (f32[3,10,800]{2,0,1:T(4,128)}, f32[3,10,800]{2,0,1:T(4,128)}, u32[]{:S(2)}, u32[]{:S(2)}) collective-permute-start(f32[3,10,800]{2,0,1:T(4,128)} %bitcast.5), channel_id=1, source_target_pairs={{0,4},{4,8},{8,12},{1,5},{5,9},{9,13},{2,6},{6,10},{10,14},{3,7},{... | collective-permute-start | bytes 288008 | tf_op jit(solution)/shard_map/ppermute | solution.py:24
  165.3 83.5 %collective-permute-start.6 = (f32[3,10,800]{2,0,1:T(4,128)}, f32[3,10,800]{2,0,1:T(4,128)}, u32[]{:S(2)}, u32[]{:S(2)}) collective-permute-start(f32[3,10,800]{2,0,1:T(4,128)} %bitcast.6), channel_id=1, source_target_pairs={{4,0},{8,4},{12,8},{5,1},{9,5},{13,9},{6,2},{10,6},{14,10},{7,3},{... | collective-permute-start | bytes 288008 | tf_op jit(solution)/shard_map/ppermute | solution.py:24
  173.9 3.8 copy-start.2
  173.9 3.8 copy-start.3

commit v2 on v1

--- a/solution.py
+++ b/solution.py
@@ -28,19 +28,59 @@
     return jnp.maximum(shell_pos * (2.0 * math.pi / azimuths), 1.0)
 
 
-def stencil_kernel(rows, below_ref, here_ref, above_ref, edge_ref, lane_ref,
-                   mag_ref, sums_ref, prev_q, prev_h, full):
+def columns_kernel(x_ref, pick_ref, out_ref):
+    for z in range(x_ref.shape[1]):
+        out_ref[0, z] = lax.dot_general(
+            pick_ref[...], x_ref[0, z], (((1,), (1,)), ((), ())),
+            precision=lax.Precision.HIGHEST, preferred_element_type=F32,
+        )
+
+
+def outer_columns(velocity, pick):
+    comps, planes, rows, width = velocity.shape
+    return pl.pallas_call(
+        columns_kernel,
+        grid=(comps, planes // 4),
+        in_specs=[
+            pl.BlockSpec((1, 4, rows, width), lambda c, z: (c, z, 0, 0)),
+            pl.BlockSpec((8, width), lambda c, z: (0, 0)),
+        ],
+        out_specs=pl.BlockSpec((1, 4, 8, rows), lambda c, z: (c, z, 0, 0)),
+        out_shape=jax.ShapeDtypeStruct((comps, planes, 8, rows), F32),
+        name="columns",
+    )(velocity, pick)
+
+
+def stencil_kernel(rows, planes, low_ref, main_ref, high_ref, left_ref, right_ref, edge_in,
+                   lane_ref, pick_ref, mag_ref, sums_ref, ring, edge_ref, prev_q, prev_h, full):
     step = pl.program_id(0)
     inv_pos = lane_ref[0:1, :]
     half_space = lane_ref[1:2, :]
     scale = lane_ref[2:3, :]
     lane = lax.broadcasted_iota(jnp.int32, (CHUNK, 128), 1)
+    above, here_slot, below = step % 3, (step + 2) % 3, (step + 1) % 3
 
     @pl.when(step == 0)
     def _():
         prev_q[...] = jnp.zeros_like(prev_q)
         prev_h[...] = jnp.zeros_like(prev_h)
         sums_ref[...] = jnp.zeros_like(sums_ref)
+
+    def take(source):
+        for c in range(3):
+            ring[above, c, PAD : PAD + rows, :] = source[c, 0]
+
+    pl.when(step < 2)(lambda: take(low_ref))
+    pl.when((step >= 2) & (step < planes + 2))(lambda: take(main_ref))
+    pl.when(step >= planes + 2)(lambda: take(high_ref))
+    for c in range(3):
+        ring[above, c, :PAD, :] = left_ref[c, 0]
+        ring[above, c, PAD + rows :, :] = right_ref[c, 0]
+        spread = lax.dot_general(
+            edge_in[c, 0], pick_ref[...], (((0,), (0,)), ((), ())),
+            precision=lax.Precision.HIGHEST, preferred_element_type=F32,
+        )
+        edge_ref[c] = spread[128 - PAD : 128 + rows + PAD]
 
     def produce(i, carry):
         base = pl.multiple_of(i * CHUNK, 8)
@@ -48,12 +88,12 @@
         out = pl.ds(base, CHUNK)
         v, dz, dt, dr = [], [], [], []
         for c in range(3):
-            wide = here_ref[c, 0, pl.ds(base, CHUNK + 16), :]
+            wide = ring[here_slot, c, pl.ds(base, CHUNK + 16), :]
             mid = wide[8 : 8 + CHUNK]
-            edge = edge_ref[c, 0, here, :]
+            edge = edge_ref[c, here, :]
             v.append(mid)
             dt.append((wide[9 : 9 + CHUNK] - wide[7 : 7 + CHUNK]) * half_space)
-            dz.append((above_ref[c, 0, here, :] - below_ref[c, 0, here, :]) * 0.5)
+            dz.append((ring[above, c, here, :] - ring[below, c, here, :]) * 0.5)
             up = jnp.where(lane == 127, edge, pltpu.roll(mid, 127, 1))
             down = jnp.where(lane == 0, edge, pltpu.roll(mid, 1, 1))
             dr.append((up - down) * 0.5)
@@ -77,7 +117,9 @@
             prev_h[f, out, :] = h
         return carry
 
-    lax.fori_loop(0, (rows + 16) // CHUNK, produce, 0)
+    @pl.when(step >= 2)
+    def _():
+        lax.fori_loop(0, (rows + 16) // CHUNK, produce, 0)
 
     def smoothed(f, base):
         wide = full[f, pl.ds(base, CHUNK + 16), :]
@@ -105,7 +147,7 @@
                 lm_o, mm_o = lm_o + lm, mm_o + mm
         return (num + (lm_d + 2.0 * lm_o), den + (mm_d + 2.0 * mm_o))
 
-    @pl.when(step >= 2)
+    @pl.when(step >= 4)
     def _():
         zero = jnp.zeros((CHUNK, 128), F32)
         num, den = lax.fori_loop(0, rows // CHUNK, consume, (zero, zero))
@@ -113,34 +155,41 @@
         sums_ref[1] += den
 
 
-def stencil(padded, edges, lanes):
-    _, deep, tall, width = padded.shape
-    rows = tall - 2 * PAD
-    steps = deep - 2
-    block = (3, 1, tall, width)
+def stencil(low, velocity, high, left, right, edges, lanes, pick):
+    _, planes, rows, width = velocity.shape
+    steps = planes + 4
+    block = (3, 1, rows, width)
+    side = pl.BlockSpec((3, 1, PAD, width), lambda j: (0, j, 0, 0))
+    small = pl.BlockSpec((8, width), lambda j: (0, 0))
     return pl.pallas_call(
-        functools.partial(stencil_kernel, rows),
+        functools.partial(stencil_kernel, rows, planes),
         grid=(steps,),
         in_specs=[
-            pl.BlockSpec(block, lambda j: (0, j, 0, 0)),
-            pl.BlockSpec(block, lambda j: (0, j + 1, 0, 0)),
-            pl.BlockSpec(block, lambda j: (0, j + 2, 0, 0)),
-            pl.BlockSpec(block, lambda j: (0, j, 0, 0)),
-            pl.BlockSpec((8, width), lambda j: (0, 0)),
+            pl.BlockSpec(block, lambda j: (0, jnp.clip(j, 0, 1), 0, 0)),
+            pl.BlockSpec(block, lambda j: (0, jnp.clip(j - 2, 0, planes - 1), 0, 0)),
+            pl.BlockSpec(block, lambda j: (0, jnp.clip(j - planes - 2, 0, 1), 0, 0)),
+            side,
+            side,
+            pl.BlockSpec((3, 1, 8, edges.shape[3]), lambda j: (0, jnp.clip(j - 2, 0, planes + 1), 0, 0)),
+            small,
+            small,
         ],
         out_specs=[
-            pl.BlockSpec((1, rows + 16, width), lambda j: (j, 0, 0)),
+            pl.BlockSpec((1, rows + 16, width), lambda j: (jnp.clip(j - 2, 0, planes + 1), 0, 0)),
             pl.BlockSpec((2, CHUNK, width), lambda j: (0, 0, 0)),
         ],
         out_shape=[
-            jax.ShapeDtypeStruct((steps, rows + 16, width), F32),
+            jax.ShapeDtypeStruct((planes + 2, rows + 16, width), F32),
             jax.ShapeDtypeStruct((2, CHUNK, width), F32),
         ],
-        scratch_shapes=[pltpu.VMEM((21, rows + 16, width), F32)] * 3,
+        scratch_shapes=[
+            pltpu.VMEM((3, 3, rows + 2 * PAD, width), F32),
+            pltpu.VMEM((3, rows + 2 * PAD, width), F32),
+        ] + [pltpu.VMEM((21, rows + 16, width), F32)] * 3,
         compiler_params=pltpu.CompilerParams(vmem_limit_bytes=58 * 2**20),
         cost_estimate=pl.CostEstimate(flops=10**9, bytes_accessed=10**8, transcendentals=0),
         name="stencil",
-    )(padded, padded, padded, edges, lanes)
+    )(low, velocity, high, left, right, edges, lanes, pick)
 
 
 def split(x):
@@ -262,8 +311,7 @@
 
 def filtered_of(velocity, far, live, scaling, wave, spread, fourier):
     comps, planes, columns, width = velocity.shape
-    fwd_hi, fwd_lo = split_table(fourier)
-    tables = (fwd_hi, fwd_lo, fwd_hi.T, fwd_lo.T)
+    tables = fourier
 
     def whole(x):
         return pl.BlockSpec(x.shape, lambda c, z: (0,) * x.ndim, pipeline_mode=pl.Buffered(1))
@@ -304,20 +352,25 @@
     turn = jnp.stack([jnp.cos(turned), jnp.sin(turned)], axis=1)
     far_shape = (parts - 1, comps, planes, 2 * NODES, width)
 
-    def gather_far(v):
-        wave, _, _ = polar_tables(cutoffs, columns, azimuths)
-        return moments(v, wave, turn, table)
-
-    sent = lax.cond(inner_side, gather_far, lambda v: jnp.zeros(far_shape, F32), velocity)
+    wave, fourier, scaling = polar_tables(cutoffs, columns, azimuths)
+    sent = lax.cond(
+        inner_side,
+        lambda v: moments(v, wave, turn, table),
+        lambda v: jnp.zeros(far_shape, F32),
+        velocity,
+    )
     far = shift_from(sent[0], "az", 1)
     for n in range(1, parts - 1):
         far = far + shift_from(sent[n], "az", n + 1)
-
-    def apply(v, f):
-        wave, fourier, scaling = polar_tables(cutoffs, columns, azimuths)
-        return filtered_of(v, f, live, scaling, wave, spread_table, fourier)
-
-    return lax.cond(inner_side, apply, lambda v, f: v, velocity, far)
+    fwd_hi, fwd_lo = split_table(fourier)
+    tables = (fwd_hi, fwd_lo, fwd_hi.T, fwd_lo.T)
+    return lax.cond(
+        inner_side,
+        lambda v, f: filtered_of(v, f, live, scaling, wave, spread_table, tables),
+        lambda v, f: v,
+        velocity,
+        far,
+    )
 
 
 def local(velocity, cutoff, shells):
@@ -329,22 +382,39 @@
     spacing = spacing_of(shell_pos, azimuths)
     scale_sq = jnp.power(spacing, 2.0 / 3.0)
 
+    left = shift_from(velocity[:, :, -PAD:], "az", -1)
+    right = shift_from(velocity[:, :, :PAD], "az", 1)
+    low = shift_from(velocity[:, -2:], "ax", -1)
+    high = shift_from(velocity[:, :2], "ax", 1)
+
+    pick = np.zeros((8, radial), np.float32)
+    pick[0, 0] = pick[1, radial - 1] = 1.0
+    pick = jnp.asarray(pick)
+    columns_out = outer_columns(velocity, pick)
+    lower = shift_from(columns_out[:, :, 1:2], "rad", -1, False)
+    upper = shift_from(columns_out[:, :, 0:1], "rad", 1, False)
+    edges = jnp.concatenate([lower, upper, jnp.zeros((3, planes, 6, columns), F32)], axis=2)
+    edges = jnp.concatenate(
+        [shift_from(edges[..., -128:], "az", -1), edges, shift_from(edges[..., :128], "az", 1)], axis=3
+    )
+    sides = jnp.concatenate([left, right], axis=2)
+    rims = (
+        low,
+        high,
+        shift_from(edges[:, -1:], "ax", -1),
+        shift_from(edges[:, :1], "ax", 1),
+        shift_from(sides[:, -2:], "ax", -1),
+        shift_from(sides[:, :2], "ax", 1),
+    )
+
     filtered = polar_step(velocity, cutoff, shells, first_shell)
-
-    low_z = shift_from(velocity[:, -2:], "ax", -1)
-    high_z = shift_from(velocity[:, :2], "ax", 1)
-    tall = jnp.concatenate([low_z, velocity, high_z], axis=1)
-    low_t = shift_from(tall[:, :, -PAD:], "az", -1)
-    high_t = shift_from(tall[:, :, :PAD], "az", 1)
-    padded = jnp.concatenate([low_t, tall, high_t], axis=2)
-    inside = padded[:, 1:-1]
-    lower = shift_from(inside[..., -1], "rad", -1, False)[..., None]
-    upper = shift_from(inside[..., 0], "rad", 1, False)[..., None]
-    lane = jnp.arange(radial)
-    edges = jnp.where(lane == 0, lower, jnp.where(lane == radial - 1, upper, 0.0))
+    filtered, low, high, edge_low, edge_high, side_low, side_high = lax.optimization_barrier((filtered,) + rims)
+    edges = jnp.concatenate([edge_low, edges, edge_high], axis=1)
+    sides = jnp.concatenate([side_low, sides, side_high], axis=1)
+    left, right = sides[:, :, :PAD], sides[:, :, PAD:]
     lanes = jnp.zeros((8, radial), F32)
     lanes = lanes.at[0].set(1.0 / shell_pos).at[1].set(0.5 / spacing).at[2].set(2.0 * scale_sq)
-    magnitude, sums = stencil(padded, edges, lanes)
+    magnitude, sums = stencil(low, velocity, high, left, right, edges, lanes, pick)
 
     totals = lax.psum(jnp.sum(sums, axis=1), ("az", "ax"))
     coefficient = totals[0] / surface_cells / (totals[1] / surface_cells + 1e-06)

time: 382 us -> 361 us (0.945)
  local copies, waits for them, and re-layouts: 47.5 us -> 15.8 us
  Pallas kernels: 173 us -> 204 us
  other arithmetic: 33.8 us -> 22.9 us
  waiting for transfers between devices: 91.7 us -> 81.2 us
  starting transfers between devices: 12.2 us -> 18.3 us
  blocking collectives: 22 us -> 17.3 us
    pallas_call x1 -> x2, Pallas kernels: 96.1 us -> 127 us  [the longest x1 116 us: stencil(): pl.pallas_call(functools.partial(stencil_kernel, rows, planes), grid=(ste...]
    slice x5, local copies, waits for them, and re-layouts: 33.4 us -> 9.73 us  [the longest x1 4.92 us: local(): high = shift_from(velocity[:, :2], 'ax', 1)]
    ppermute x7 -> x13, waiting for transfers between devices: 91.7 us -> 81.2 us  [shift_from(): return lax.ppermute(block, axis, pairs)]
    select_n x1 -> x0, other arithmetic: 8.65 us -> none  [local(): jnp.where(lane == 0, lower, jnp.where(lane == radial - 1, upper, 0.0))]
    unnamed x10 -> x17, local copies, waits for them, and re-layouts: 8.17 us -> 1.65 us
    ppermute x7 -> x13, starting transfers between devices: 12.2 us -> 18.3 us  [shift_from(): return lax.ppermute(block, axis, pairs)]
    psum x1, blocking collectives: 22 us -> 17.3 us  [local(): totals = lax.psum(jnp.sum(sums, axis=1), ('az', 'ax'))]
  transfers between devices with their start and end apart: 7 -> 13, of which waited for: 4 -> 4; matrix products, arithmetic and copies ran while one was open for 16% -> 7% of each run, Pallas kernels for 20% -> 21%
where the time goes in v2:
time: 361 us; the launch traced here: 360 us
  Pallas kernels  204 us (57%)
  waiting for transfers between devices  81.2 us (22%)
  other arithmetic  22.9 us (6%)
  starting transfers between devices  18.3 us (5%)
  blocking collectives  17.3 us (5%)
  local copies, waits for them, and re-layouts  15.8 us (4%)
    pallas_call x1, Pallas kernels, stencil(): pl.pallas_call(functools.partial(stencil_kernel, rows, planes), grid=(ste...  116 us
    ppermute x13, waiting for transfers between devices, shift_from(): return lax.ppermute(block, axis, pairs)  81.2 us
    pallas_call x1, Pallas kernels, filtered_of(): pl.pallas_call(filter_kernel, grid=(comps, planes // 2), in_specs=[block,...  65.8 us
    ppermute x13, starting transfers between devices, shift_from(): return lax.ppermute(block, axis, pairs)  18.3 us
    psum x1, blocking collectives, local(): totals = lax.psum(jnp.sum(sums, axis=1), ('az', 'ax'))  17.3 us
    pallas_call x1, Pallas kernels, moments(): pl.pallas_call(moment_kernel, grid=(comps, planes // 2), in_specs=[pl.Blo...  11.4 us
    pallas_call x1, Pallas kernels, outer_columns(): pl.pallas_call(columns_kernel, grid=(comps, planes // 4), in_specs=[pl.Bl...  10.4 us
  transfers between devices with their start and end apart: 13, of which 4 were waited for; matrix products, arithmetic and copies ran while one was open for 7% of the time, Pallas kernels for 21%

profile of v2, /device:TPU:0, one launch (start us, length us, event | category | flops | bytes accessed | tf_op | source)
XLA Modules:
  0.0 360.4 jit_solution(18297693782471584522)
XLA Ops:
  3.3 11.4 %conditional.2 = (f32[1,3,8,96,128]{4,3,2,1,0:T(8,128)}) conditional(s32[]{:T(128)} %convert_element_type.59, () %tuple.33, (f32[3,8,768,128]{3,2,1,0:T(8,128)}, f32[2,768,128]{2,1,0:T(8,128)S(1)}, f32[1,2,128]{2,1,0:T(2,128)S(1)}, bf16[1,96,768]{2,1,0:T(8,128)(2,1)S(1)}) %tuple.58), branch_computations={%region_0.1_spmd, %region_1.2_spmd} | conditional | bytes 1179660 | solution.py:356
  3.3 11.4 %moments.1 = f32[1,3,8,96,128]{4,3,2,1,0:T(8,128)} custom-call(f32[3,8,768,128]{3,2,1,0:T(8,128)} %get-tuple-element.71.x_ref, f32[2,768,128]{2,1,0:T(8,128)S(1)} %get-tuple-element.72.wave_ref, f32[1,2,128]{2,1,0:T(2,128)S(1)} %get-tuple-element.73.turn_ref, bf16[1,96,768]{2,1,0:T(8,128)(2,1)S(1)} %get-tuple-element.74.table_ref), custom_call_target="tpu_custom_call" | custom-call | tf_op jit(solution)/shard_map/cond/branch_1_fun/moments/pallas_call | solution.py:297
  14.7 3.0 collective-permute-start
  17.7 10.4 %columns.1 = f32[3,8,8,768]{3,2,1,0:T(8,128)} custom-call(f32[3,8,768,128]{3,2,1,0:T(8,128)} %main_ref.1, f32[8,128]{1,0:T(8,128)} %constant.173.clone.pick_ref), custom_call_target="tpu_custom_call" | custom-call | tf_op jit(solution)/shard_map/columns/pallas_call | solution.py:41
  32.3 4.9 %fusion.24 = (f32[3,2,768,128]{3,2,1,0:T(8,128)}, f32[3,2,768,128]{3,2,1,0:T(8,128)}) fusion(f32[3,8,768,128]{3,2,1,0:T(8,128)} %main_ref.1), kind=kLoop, calls=%fused_computation.64 | loop fusion | bytes 9437184 | tf_op jit(solution)/shard_map/slice | solution.py:388
  38.8 2.2 collective-permute-start.2
  41.9 1.8 fusion.23
  43.7 6.3 %fusion.6 = (f32[512,768]{1,0:T(8,128)S(1)}, f32[512,768]{1,0:T(8,128)S(1)}) fusion(s32[768]{0:T(1024)S(1)} %broadcast_multiply_fusion), kind=kLoop, calls=%fused_computation.12 | loop fusion | flops 3538944 | bytes 3148800 | tf_op jit(solution)/shard_map/cos | solution.py:288
  51.7 2.6 copy.9
  54.3 1.7 copy.10
  57.0 1.7 collective-permute-start.5
  58.8 6.9 %collective-permute-done.5 = f32[3,8,8,128]{3,2,1,0:T(8,128)S(1)} collective-permute-done((f32[3,8,8,128]{3,2,1,0:T(8,128)S(1)}, f32[3,8,8,128]{3,2,1,0:T(8,128)S(1)}, u32[]{:S(2)}, u32[]{:S(2)}) %collective-permute-start.5) | collective-permute-done | bytes 98336 | tf_op jit(solution)/shard_map/ppermute | solution.py:24
  66.3 4.2 %collective-permute-done.6 = f32[3,8,8,128]{3,2,1,0:T(8,128)S(1)} collective-permute-done((f32[3,8,8,128]{3,2,1,0:T(8,128)}, f32[3,8,8,128]{3,2,1,0:T(8,128)S(1)}, u32[]{:S(2)}, u32[]{:S(2)}) %collective-permute-start.6) | collective-permute-done | bytes 98336 | tf_op jit(solution)/shard_map/ppermute | solution.py:24
  73.6 3.1 collective-permute-done.10
  76.7 1.7 collective-permute-start.8
  79.1 66.9 %collective-permute-done.7 = f32[3,1,8,1024]{3,2,1,0:T(8,128)} collective-permute-done((f32[3,1,8,1024]{3,2,1,0:T(8,128)S(1)}, f32[3,1,8,1024]{3,2,1,0:T(8,128)}, u32[]{:S(2)}, u32[]{:S(2)}) %collective-permute-start.7) | collective-permute-done | bytes 98336 | tf_op jit(solution)/shard_map/ppermute | solution.py:24
  146.0 3.8 %collective-permute-start.12 = (f32[3,2,32,128]{3,2,1,0:T(8,128)}, f32[3,2,32,128]{3,2,1,0:T(8,128)}, u32[]{:S(2)}, u32[]{:S(2)}) collective-permute-start(f32[3,2,32,128]{3,2,1,0:T(8,128)} %get-tuple-element.125), channel_id=1, source_target_pairs={{1,0},{2,1},{3,2},{0,3},{5,4},{6,5},{7,6},{4,7},{9,8},{10,9},{11,1... | collective-permute-start | bytes 294920 | tf_op jit(solution)/shard_map/ppermute | solution.py:24
  149.8 1.9 pad_maximum_fusion.4
  151.7 65.8 %conditional.3 = (f32[3,8,768,128]{3,2,1,0:T(8,128)}) conditional(s32[]{:T(128)} %convert_element_type.59, f32[3,8,768,128]{3,2,1,0:T(8,128)} %main_ref.1, (f32[3,8,768,128]{3,2,1,0:T(8,128)}, f32[3,8,96,128]{3,2,1,0:T(8,128)}, f32[3,1,128]{2,1,0:T(1,128)S(1)}, f32[1024,128]{1,0:T(8,128)}, f32[2,768,128]{2,1,0:T(8,128)S(1)}, ...), branch_computations={%region_2.3_spmd, %region_3.4_spmd} | conditional | flops 30000001024 | bytes 20000008 | solution.py:367
  151.7 65.8 %polar.1 = f32[3,8,768,128]{3,2,1,0:T(8,128)} custom-call(f32[3,8,768,128]{3,2,1,0:T(8,128)} %get-tuple-element.75.x_ref, f32[3,8,96,128]{3,2,1,0:T(8,128)} %get-tuple-element.76.far_ref, f32[3,1,128]{2,1,0:T(1,128)S(1)} %get-tuple-element.77.live_ref, f32[1024,128]{1,0:T(8,128)} %get-tuple-element.78.scaling_ref, ...), custom_call_target="tpu_custom_call" | custom-call | flops 30000001024 | bytes 20000000 | tf_op jit(solution)/shard_map/cond/branch_1_fun/polar/pallas_call | solution.py:320
  219.5 2.1 pad_maximum_fusion.1.edge_in
  221.6 116.5 %stencil.1 = (f32[10,784,128]{2,1,0:T(8,128)}, f32[2,16,128]{2,1,0:T(8,128)}) custom-call(f32[3,2,768,128]{3,2,1,0:T(8,128)} %collective-permute-done.1.low_ref, f32[3,8,768,128]{3,2,1,0:T(8,128)} %main_ref.1, f32[3,2,768,128]{3,2,1,0:T(8,128)} %collective-permute-done.2.high_ref, f32[3,12,16,128]{3,2,1,0:T(8,128)} %get-tuple-element.122.left_ref, ...), custom_call_target="tpu_custom_call" | custom-call | flops 1000000000 | bytes 100000000 | tf_op jit(solution)/shard_map/stencil/pallas_call | solution.py:164
  338.8 17.3 %psum.7 = f32[2,128]{1,0:T(2,128)S(1)} all-reduce(f32[2,128]{1,0:T(2,128)S(1)} %reduce_sum.9), channel_id=1, replica_groups=mesh['az'=2,'rad'=4,'ax'=4] {'az','ax'}, use_global_device_ids=true, to_apply=%region_5.6 | all-reduce | flops 256 | bytes 2048 | tf_op jit(solution)/shard_map/psum | solution.py:419
  356.6 3.8 %slice_multiply_fusion = f32[8,768,128]{2,1,0:T(8,128)} fusion(f32[10,784,128]{2,1,0:T(8,128)} %get-tuple-element.105, f32[128]{0:T(128)S(1)} %get-tuple-element.106), kind=kLoop, calls=%fused_computation.4 | loop fusion | flops 786432 | bytes 6291968 | tf_op jit(solution)/shard_map/mul | solution.py:421
  (62 shorter events, 19.6 us)
Async XLA Ops:
  0.6 2.7 copy-start.5
  14.7 131.3 %collective-permute-start = (f32[3,8,96,128]{3,2,1,0:T(8,128)}, f32[3,8,96,128]{3,2,1,0:T(8,128)}, u32[]{:S(2)}, u32[]{:S(2)}) collective-permute-start(f32[3,8,96,128]{3,2,1,0:T(8,128)} %bitcast.2), channel_id=1, source_target_pairs={{16,0},{0,16},{17,1},{1,17},{18,2},{2,18},{19,3},{3,19},{20,4},{4,... | collective-permute-start | bytes 3538952 | tf_op jit(solution)/shard_map/ppermute | solution.py:24
  29.5 26.5 %collective-permute-start.3 = (f32[3,8,1,768]{3,2,1,0:T(1,128)S(1)}, f32[3,8,1,768]{3,2,1,0:T(1,128)S(1)}, u32[]{:S(2)}, u32[]{:S(2)}) collective-permute-start(f32[3,8,1,768]{3,2,1,0:T(1,128)S(1)} %get-tuple-element.123), channel_id=1, source_target_pairs={{0,4},{4,8},{8,12},{1,5},{5,9},{9,13},{2,6},{6,10},{10,14},{3,7},{... | collective-permute-start | bytes 221192 | tf_op jit(solution)/shard_map/ppermute | solution.py:24
  31.0 25.3 %collective-permute-start.4 = (f32[3,8,1,768]{3,2,1,0:T(1,128)S(1)}, f32[3,8,1,768]{3,2,1,0:T(1,128)S(1)}, u32[]{:S(2)}, u32[]{:S(2)}) collective-permute-start(f32[3,8,1,768]{3,2,1,0:T(1,128)S(1)} %get-tuple-element.124), channel_id=1, source_target_pairs={{4,0},{8,4},{12,8},{5,1},{9,5},{13,9},{6,2},{10,6},{14,10},{7,3},{... | collective-permute-start | bytes 221192 | tf_op jit(solution)/shard_map/ppermute | solution.py:24
  37.2 180.4 %collective-permute-start.1 = (f32[3,2,768,128]{3,2,1,0:T(8,128)}, f32[3,2,768,128]{3,2,1,0:T(8,128)}, u32[]{:S(2)}, u32[]{:S(2)}) collective-permute-start(f32[3,2,768,128]{3,2,1,0:T(8,128)} %get-tuple-element.114), channel_id=1, source_target_pairs={{3,0},{0,1},{1,2},{2,3},{7,4},{4,5},{5,6},{6,7},{11,8},{8,9},{9,10... | collective-permute-start | bytes 7077896 | tf_op jit(solution)/shard_map/ppermute | solution.py:24
  38.8 178.8 %collective-permute-start.2 = (f32[3,2,768,128]{3,2,1,0:T(8,128)}, f32[3,2,768,128]{3,2,1,0:T(8,128)}, u32[]{:S(2)}, u32[]{:S(2)}) collective-permute-start(f32[3,2,768,128]{3,2,1,0:T(8,128)} %get-tuple-element.113), channel_id=1, source_target_pairs={{1,0},{2,1},{3,2},{0,3},{5,4},{6,5},{7,6},{4,7},{9,8},{10,9},{11,1... | collective-permute-start | bytes 7077896 | tf_op jit(solution)/shard_map/ppermute | solution.py:24
  43.7 6.3 %copy-start.7 = (s32[3]{0:T(128)S(1)}, s32[3]{0:T(128)}, u32[]{:S(2)}) copy-start(s32[3]{0:T(128)} %param.18) | copy-start | bytes 40
  56.0 16.0 %collective-permute-start.9 = (f32[3,8,16,128]{3,2,1,0:T(8,128)}, f32[3,8,16,128]{3,2,1,0:T(8,128)S(1)}, u32[]{:S(2)}, u32[]{:S(2)}) collective-permute-start(f32[3,8,16,128]{3,2,1,0:T(8,128)} %get-tuple-element.112), channel_id=1, source_target_pairs={{16,0},{0,16},{17,1},{1,17},{18,2},{2,18},{19,3},{3,19},{20,4},{4,... | collective-permute-start | bytes 589832 | tf_op jit(solution)/shard_map/ppermute | solution.py:24
  57.0 8.7 %collective-permute-start.5 = (f32[3,8,8,128]{3,2,1,0:T(8,128)S(1)}, f32[3,8,8,128]{3,2,1,0:T(8,128)S(1)}, u32[]{:S(2)}, u32[]{:S(2)}) collective-permute-start(f32[3,8,8,128]{3,2,1,0:T(8,128)S(1)} %get-tuple-element.119), channel_id=1, source_target_pairs={{16,0},{0,16},{17,1},{1,17},{18,2},{2,18},{19,3},{3,19},{20,4},{4,... | collective-permute-start | bytes 294920 | tf_op jit(solution)/shard_map/ppermute | solution.py:24
  65.7 6.3 %copy-start = (f32[3,8,8,128]{3,2,1,0:T(8,128)}, f32[3,8,8,128]{3,2,1,0:T(8,128)S(1)}, u32[]{:S(2)}) copy-start(f32[3,8,8,128]{3,2,1,0:T(8,128)S(1)} %collective-permute-done.5) | copy-start | bytes 294916
  65.7 4.8 %collective-permute-start.6 = (f32[3,8,8,128]{3,2,1,0:T(8,128)}, f32[3,8,8,128]{3,2,1,0:T(8,128)S(1)}, u32[]{:S(2)}, u32[]{:S(2)}) collective-permute-start(f32[3,8,8,128]{3,2,1,0:T(8,128)} %get-tuple-element.120), channel_id=1, source_target_pairs={{16,0},{0,16},{17,1},{1,17},{18,2},{2,18},{19,3},{3,19},{20,4},{4,... | collective-permute-start | bytes 294920 | tf_op jit(solution)/shard_map/ppermute | solution.py:24
  66.3 85.4 %copy-start.6 = (f32[8,128]{1,0:T(8,128)}, f32[8,128]{1,0:T(8,128)S(1)}, u32[]{:S(2)}) copy-start(f32[8,128]{1,0:T(8,128)S(1)} %scatter.14.lane_ref) | copy-start | bytes 12292
  70.5 1.4 copy-start.2
  70.5 6.1 %collective-permute-start.10 = (f32[3,8,16,128]{3,2,1,0:T(8,128)}, f32[3,8,16,128]{3,2,1,0:T(8,128)S(1)}, u32[]{:S(2)}, u32[]{:S(2)}) collective-permute-start(f32[3,8,16,128]{3,2,1,0:T(8,128)} %get-tuple-element.111), channel_id=1, source_target_pairs={{16,0},{0,16},{17,1},{1,17},{18,2},{2,18},{19,3},{3,19},{20,4},{4,... | collective-permute-start | bytes 589832 | tf_op jit(solution)/shard_map/ppermute | solution.py:24
  72.0 0.7 copy-start.4
  72.7 73.4 %collective-permute-start.7 = (f32[3,1,8,1024]{3,2,1,0:T(8,128)S(1)}, f32[3,1,8,1024]{3,2,1,0:T(8,128)}, u32[]{:S(2)}, u32[]{:S(2)}) collective-permute-start(f32[3,1,8,1024]{3,2,1,0:T(8,128)S(1)} %get-tuple-element.118), channel_id=1, source_target_pairs={{3,0},{0,1},{1,2},{2,3},{7,4},{4,5},{5,6},{6,7},{11,8},{8,9},{9,10... | collective-permute-start | bytes 294920 | tf_op jit(solution)/shard_map/ppermute | solution.py:24
  76.7 140.9 %collective-permute-start.8 = (f32[3,1,8,1024]{3,2,1,0:T(8,128)}, f32[3,1,8,1024]{3,2,1,0:T(8,128)}, u32[]{:S(2)}, u32[]{:S(2)}) collective-permute-start(f32[3,1,8,1024]{3,2,1,0:T(8,128)} %get-tuple-element.117), channel_id=1, source_target_pairs={{1,0},{2,1},{3,2},{0,3},{5,4},{6,5},{7,6},{4,7},{9,8},{10,9},{11,1... | collective-permute-start | bytes 294920 | tf_op jit(solution)/shard_map/ppermute | solution.py:24
  146.0 71.6 %collective-permute-start.11 = (f32[3,2,32,128]{3,2,1,0:T(8,128)}, f32[3,2,32,128]{3,2,1,0:T(8,128)}, u32[]{:S(2)}, u32[]{:S(2)}) collective-permute-start(f32[3,2,32,128]{3,2,1,0:T(8,128)} %get-tuple-element.126), channel_id=1, source_target_pairs={{3,0},{0,1},{1,2},{2,3},{7,4},{4,5},{5,6},{6,7},{11,8},{8,9},{9,10... | collective-permute-start | bytes 294920 | tf_op jit(solution)/shard_map/ppermute | solution.py:24
  146.0 71.6 %collective-permute-start.12 = (f32[3,2,32,128]{3,2,1,0:T(8,128)}, f32[3,2,32,128]{3,2,1,0:T(8,128)}, u32[]{:S(2)}, u32[]{:S(2)}) collective-permute-start(f32[3,2,32,128]{3,2,1,0:T(8,128)} %get-tuple-element.125), channel_id=1, source_target_pairs={{1,0},{2,1},{3,2},{0,3},{5,4},{6,5},{7,6},{4,7},{9,8},{10,9},{11,1... | collective-permute-start | bytes 294920 | tf_op jit(solution)/shard_map/ppermute | solution.py:24
  217.6 2.0 copy-start.1
  217.6 2.0 copy-start.3
